TPU v7x, 32 devices: a whole 2x2x4 slice. The times are simulated.
32 devices in a mesh: groups: 2 (over x), ctx: 16 (over z, y, core).
Axes of the slice: x: 2, y: 2, z: 4, core: 2. Of those that a mesh axis runs over, the one named last changes fastest.
Arguments:
- frames: bfloat16 [32, 384, 1024], P('groups', 'ctx'), parts along dimension 0, may hold values from -6 to 6
- grad_out: bfloat16 [12288, 1024], P(('groups', 'ctx')), parts along dimension 0, may hold values from -6 to 6
- valid_count: int32 [2], P('groups'), parts along dimension 0, may hold values from 3072 to 6144
- norm_gain: float32 [1024], replicated, may hold values from 0.1 to 1.9
- w_in: bfloat16 [2048, 1024], P('ctx'), may hold values from -0.1875 to 0.1875
- depth_weight: bfloat16 [1024, 31], replicated, may hold values from -1 to 1
- depth_gain: float32 [1024], replicated, may hold values from 0.1 to 1.9
- w_out: bfloat16 [1024, 1024], P('ctx'), may hold values from -0.1875 to 0.1875
Outputs:
- output: bfloat16 [12288, 1024], P(('groups', 'ctx')), parts along dimension 0
- grad_frames: bfloat16 [32, 384, 1024], P('groups', 'ctx'), parts along dimension 0
- grad_w_in: float32 [4096, 1024], P(('groups', 'ctx')), parts along dimension 0
- grad_w_out: float32 [2048, 1024], P(('groups', 'ctx')), parts along dimension 0
- grad_depth: float32 [2048, 31], P('groups'), parts along dimension 0
- grad_gains: float32 [4, 1024], P('groups'), parts along dimension 0
There are 2 independent parts, one for each index of `groups`. A program takes and returns all parts, laid end to end along the dimension named above; an argument that names none is the same for every part. Nothing has to cross between parts.
Inputs may be any that keep to these rules, and one draw needn't show every extreme that they name: frames from index valid_count[0] on are padding.
All inputs are finite; a program needn't handle non-finite values.
Results may differ from a plain program's by a relative error of at most 0.0069.
Values may be sent and summed in bfloat16 or wider, within the bound.
A program may use at most 128 MiB of HBM per device.

v0:
```python
import jax
import jax.numpy as jnp
from jax import lax
from jax.sharding import PartitionSpec as P

epsilon = 1e-05


def extended(block, sides, width):
    for axis, dim in sides:
        count = lax.axis_size(axis)
        forward = [(i, i + 1) for i in range(count - 1)]
        backward = [(target, source) for source, target in forward]
        low = lax.ppermute(
            lax.slice_in_dim(block, block.shape[dim] - width, None, axis=dim), axis, forward
        )
        high = lax.ppermute(lax.slice_in_dim(block, 0, width, axis=dim), axis, backward)
        block = jnp.concatenate([low, block, high], axis=dim)
    return block


def normalize(values):
    center = jnp.mean(values, axis=-1, keepdims=True)
    shifted = values - center
    inverse = lax.rsqrt(jnp.mean(shifted * shifted, axis=-1, keepdims=True) + epsilon)
    return (shifted * inverse, inverse)


def norm_backward(upstream, normed, inverse):
    first = jnp.mean(upstream, axis=-1, keepdims=True)
    second = jnp.mean(upstream * normed, axis=-1, keepdims=True)
    return (upstream - first - normed * second) * inverse


def frame_sum(left, right):
    return lax.dot_general(
        left, right, (((0,), (0,)), ((), ())), preferred_element_type=jnp.float32
    )


def times_transposed(left, right):
    return lax.dot_general(
        left, right, (((1,), (1,)), ((), ())), preferred_element_type=jnp.float32
    )


def depthwise(padded, kernel, length):
    total = padded[0:length] * kernel[:, 0]
    for offset in range(1, kernel.shape[1]):
        total = total + padded[offset : offset + length] * kernel[:, offset]
    return total


def depthwise_back(padded, kernel, length):
    taps = kernel.shape[1]
    total = padded[taps - 1 : taps - 1 + length] * kernel[:, 0]
    for offset in range(1, taps):
        begin = taps - 1 - offset
        total = total + padded[begin : begin + length] * kernel[:, offset]
    return total


def shards(frames, grad_out, valid_count, norm_gain, w_in, depth_weight, depth_gain, w_out):
    span = lax.axis_size("ctx")
    ordered = lax.all_to_all(frames, "ctx", split_axis=0, concat_axis=1, tiled=True)
    local_frames = ordered.shape[1]
    width = ordered.shape[2]
    taps = depth_weight.shape[1]
    margin = (taps - 1) // 2
    scale = (local_frames * span) ** (-0.5)
    inputs = ordered.reshape(local_frames, width)
    positions = lax.axis_index("ctx") * local_frames + lax.iota(jnp.int32, local_frames)
    keep = (positions < valid_count[0]).astype(jnp.float32)[:, None]
    wide_in = inputs.astype(jnp.float32)
    normed_in, inverse_in = normalize(wide_in)
    scaled_in = (normed_in * norm_gain).astype(jnp.bfloat16)
    projected = times_transposed(scaled_in, lax.all_gather(w_in, "ctx", axis=0, tiled=True))
    linear = projected[:, :width]
    sigma = jax.nn.sigmoid(projected[:, width:])
    glu = (linear * sigma * keep).astype(jnp.bfloat16)
    padded = extended(glu, (("ctx", 0),), margin).astype(jnp.float32)
    kernel = depth_weight.astype(jnp.float32)
    conv = depthwise(padded, kernel, local_frames)
    normed_conv, inverse_conv = normalize(conv)
    gained = normed_conv * depth_gain
    sig_two = jax.nn.sigmoid(gained)
    act = (gained * sig_two * keep).astype(jnp.bfloat16)
    mixed = times_transposed(act, lax.all_gather(w_out, "ctx", axis=0, tiled=True))
    output = (wide_in + mixed).astype(jnp.bfloat16)
    grad_w_out = (
        lax.psum_scatter(frame_sum(grad_out, act), "ctx", scatter_dimension=0, tiled=True) * scale
    )
    columns = grad_out
    grad_act = jnp.dot(
        columns,
        lax.all_gather(w_out, "ctx", axis=0, tiled=True),
        preferred_element_type=jnp.float32,
    )
    grad_gained = grad_act * keep * (sig_two * (1.0 + gained * (1.0 - sig_two)))
    grad_conv = norm_backward(grad_gained * depth_gain, normed_conv, inverse_conv).astype(
        jnp.bfloat16
    )
    grad_pad = extended(grad_conv, (("ctx", 0),), margin).astype(jnp.float32)
    grad_glu = depthwise_back(grad_pad, kernel, local_frames) * keep
    grad_wide = grad_conv.astype(jnp.float32)
    depth_local = jnp.stack(
        [
            jnp.sum(grad_wide * padded[offset : offset + local_frames], axis=0)
            for offset in range(taps)
        ],
        axis=1,
    )
    grad_projected = jnp.concatenate(
        [grad_glu * sigma, grad_glu * linear * sigma * (1.0 - sigma)], axis=1
    ).astype(jnp.bfloat16)
    grad_w_in = (
        lax.psum_scatter(
            frame_sum(grad_projected, scaled_in), "ctx", scatter_dimension=0, tiled=True
        )
        * scale
    )
    columns = grad_projected
    grad_scaled = jnp.dot(
        columns, lax.all_gather(w_in, "ctx", axis=0, tiled=True), preferred_element_type=jnp.float32
    )
    grad_in = norm_backward(grad_scaled * norm_gain, normed_in, inverse_in)
    gains_local = jnp.stack(
        [jnp.sum(grad_scaled * normed_in, axis=0), jnp.sum(grad_gained * normed_conv, axis=0)],
        axis=0,
    )
    depth_total, gains_total = lax.psum((depth_local, gains_local), "ctx")
    grad_local = (
        (grad_out.astype(jnp.float32) + grad_in)
        .astype(jnp.bfloat16)
        .reshape(1, local_frames, width)
    )
    grad_frames = lax.all_to_all(grad_local, "ctx", split_axis=1, concat_axis=0, tiled=True)
    return (output, grad_frames, grad_w_in, grad_w_out, depth_total * scale, gains_total * scale)


def solution(mesh):
    placed = (
        P("groups", "ctx", None),
        P(("groups", "ctx"), None),
        P("groups"),
        P(),
        P("ctx", None),
        P(),
        P(),
        P("ctx", None),
    )
    return jax.shard_map(
        shards,
        mesh=mesh,
        in_specs=placed,
        out_specs=(
            P(("groups", "ctx"), None),
            P("groups", "ctx", None),
            P(("groups", "ctx"), None),
            P(("groups", "ctx"), None),
            P("groups", None),
            P("groups", None),
        ),
        check_vma=False,
    )
```

profile of v0, /device:TPU:0, one launch (start us, length us, event | category | flops | bytes accessed | tf_op | source)
XLA Modules:
  0.0 406.9 jit_solution(13693910208653127402)
XLA Ops:
  7.9 7.4 %all-to-all-start = ((bf16[16,24,1024]{2,1,0:T(8,128)(2,1)}), bf16[16,24,1024]{2,1,0:T(8,128)(2,1)S(1)}, u32[]{:S(2)}, u32[]{:S(2)}) async-start(bf16[16,24,1024]{2,1,0:T(8,128)(2,1)} %param.8), calls=%async_computation | async-start | bytes 1572864 | tf_op jit(solution)/shard_map/all_to_all | solution.py:65
  16.9 24.8 %all-to-all-done = bf16[16,24,1024]{2,1,0:T(8,128)(2,1)S(1)} async-done(((bf16[16,24,1024]{2,1,0:T(8,128)(2,1)}), bf16[16,24,1024]{2,1,0:T(8,128)(2,1)S(1)}, u32[]{:S(2)}, u32[]{:S(2)}) %all-to-all-start) | async-done | bytes 786464 | tf_op jit(solution)/shard_map/all_to_all | solution.py:65
  42.7 27.8 %all-gather.3.cloned.1.call-done = bf16[2048,1024]{1,0:T(8,128)(2,1)} async-done(((bf16[128,1024]{1,0:T(8,128)(2,1)}), bf16[2048,1024]{1,0:T(8,128)(2,1)}) %all-gather.3.cloned.1.call-update) | async-done | bytes 4194320 | tf_op jit(solution)/shard_map/all_gather | solution.py:77
  70.5 4.0 fusion.91
  76.3 2.2 collective-permute-start
  81.8 7.2 %fusion.86 = (f32[384]{0:T(512)S(1)}, f32[384,1024]{1,0:T(8,128)S(1)}) fusion(f32[1024]{0:T(1024)S(1)} %bitcast.176, f32[414,1024]{1,0:T(8,128)S(1)} %maximum_convert_fusion, f32[1024]{0:T(1024)S(1)} %bitcast.174, f32[1024]{0:T(1024)S(1)} %bitcast.172, f32[1024]{0:T(1024)S(1)} %bitcast.170, f32[1024]{0:T(1024)S(1)} %bitcast.168, f32[1024]{0:T(1024)S(1)} %bitcast.166, ...), kind=kLoop, calls=%fused_computation.184 | loop fusion | flops 24379008 | bytes 50460160 | tf_op jit(solution)/shard_map/reduce_sum | solution.py:23
  89.4 23.3 %all-gather.5.cloned.1.call-done = bf16[1024,1024]{1,0:T(8,128)(2,1)} async-done(((bf16[64,1024]{1,0:T(8,128)(2,1)}), bf16[1024,1024]{1,0:T(8,128)(2,1)}) %all-gather.5.cloned.1.call-update) | async-done | bytes 2097168 | tf_op jit(solution)/shard_map/all_gather | solution.py:88
  112.7 4.1 %multiply_reduce_fusion = (f32[1024]{0:T(1024)}, f32[384]{0:T(512)S(1)}, f32[384]{0:T(512)S(1)}, f32[384,1024]{1,0:T(8,128)S(1)}) fusion(f32[384,1024]{1,0:T(8,128)S(1)} %get-tuple-element.65, f32[384]{0:T(512)S(1)} %add_rsqrt_fusion.1, f32[384]{0:T(512)S(1)} %broadcast_multiply_fusion.9, f32[1024]{0:T(1024)S(1)} %copy-done.17, f32[384]{0:T(512)S(1)} %fusion.82, ...), kind=kOutput, calls=%fused_computation.149 | convolution fusion | flops 812382464 | bytes 6045184 | tf_op jit(solution)/shard_map/dot_general | solution.py:94
  116.8 4.5 %fusion.30 = (f32[1024]{0:T(1024)S(1)}, f32[1024]{0:T(1024)S(1)}, f32[1024]{0:T(1024)S(1)}, f32[1024]{0:T(1024)S(1)}, f32[1024]{0:T(1024)S(1)}, /*index=5*/f32[1...) fusion(f32[414,1024]{1,0:T(8,128)S(1)} %maximum_convert_fusion,, ...), kind=kLoop, calls=%fused_computation.62 | loop fusion | flops 17676288 | bytes 32327680 | tf_op jit(solution)/shard_map/reduce_sum | solution.py:108
  121.3 2.6 fusion.29
  124.0 2.7 stack.136
  126.9 4.6 %convolution_bitcast_fusion = f32[1024,1024]{0,1:T(8,128)} fusion(bf16[384,1024]{1,0:T(8,128)(2,1)} %param.9, f32[384,1024]{1,0:T(8,128)S(1)} %get-tuple-element.65, f32[1024]{0:T(1024)} %param.14, f32[384]{0:T(512)S(1)} %add_rsqrt_fusion.1, f32[384]{0:T(512)S(1)} %broadcast_multiply_fusion.9, f32[384]{0:T(512)S(1)} %fusion.82), kind=kOutput, calls=%fused_computation.31 | convolution fusion | flops 808845312 | bytes 6562304 | tf_op jit(solution)/shard_map/dot_general | solution.py:36
  131.5 5.4 %copy.19 = f32[1024,1024]{1,0:T(8,128)} copy(f32[1024,1024]{0,1:T(8,128)} %convolution_bitcast_fusion) | data formatting | bytes 8388608
  137.9 2.2 collective-permute-start.2
  144.6 6.7 %multiply_convert_fusion.1 = (bf16[384,1024]{1,0:T(8,128)(2,1)S(1)}, f32[384,1024]{1,0:T(8,128)S(1)}) fusion(f32[384,2048]{1,0:T(8,128)S(1)} %copy-done.1, f32[384]{0:T(512)S(1)} %fusion.82, f32[1024]{0:T(1024)S(1)} %bitcast.177, f32[414,1024]{1,0:T(8,128)S(1)} %maximum_convert_fusion.1, f32[1024]{0:T(1024)S(1)} %bitcast.175, f32[1024]{0:T(1024)S(1)} %bitcast.173, ...), kind=kLoop, calls=%fused_computation.151 | loop fusion | flops 26345472 | bytes 52819456 | tf_op jit(solution)/shard_map/convert.1
  152.9 5.6 %fusion.80 = f32[2048,1024]{1,0:T(8,128)} fusion(bf16[384,1024]{1,0:T(8,128)(2,1)S(1)} %copy-done.8, bf16[384,1024]{1,0:T(8,128)(2,1)S(1)} %multiply_convert_fusion, bf16[384,1024]{1,0:T(8,128)(2,1)S(1)} %get-tuple-element.62), kind=kOutput, calls=%fused_computation.163 | convolution fusion | flops 1613758464 | bytes 10747904 | tf_op jit(solution)/shard_map/dot_general | solution.py:36
  160.1 4.4 %fusion.78 = (f32[1024]{0:T(1024)S(1)}, f32[384]{0:T(512)S(1)}, f32[384]{0:T(512)S(1)}, f32[384,1024]{1,0:T(8,128)S(1)}) fusion(bf16[16,24,1024]{2,1,0:T(8,128)(2,1)S(1)} %copy-done.3, f32[384]{0:T(512)S(1)} %rsqrt.20, f32[384]{0:T(512)S(1)} %div.33, f32[1024]{0:T(1024)S(1)} %copy-done.15, bf16[2048,1024]{1,0:T(8,128)(2,1)} %all-gather.3.cloned.1.call-done, ...), kind=kOutput, calls=%fused_computation.147 | convolution fusion | flops 1617295616 | bytes 8140800 | tf_op jit(solution)/shard_map/dot_general | solution.py:123
  166.9 5.2 %reduce.8 = bf16[384,1024]{1,0:T(8,128)(2,1)S(1)} reduce(bf16[384,1,1024]{2,1,0:T(2,128)(2,1)S(1)} %bitcast.112, bf16[]{:T(256)} %broadcast.118), dimensions={1}, to_apply=%bitcast.110.reduce_sub_computation | reduce | bytes 1572866
  173.5 7.4 %all-to-all-start.1 = ((bf16[16,2,12288]{2,1,0:T(2,128)(2,1)}), bf16[16,2,12288]{2,1,0:T(2,128)(2,1)S(1)}, u32[]{:S(2)}, u32[]{:S(2)}) async-start(bf16[16,2,12288]{2,1,0:T(2,128)(2,1)} %reshape.139), calls=%async_computation.1 | async-start | bytes 1572864 | tf_op jit(solution)/shard_map/all_to_all | solution.py:137
  181.0 3.7 fusion.79
  184.7 37.9 %psum.15 = f32[2,1024]{1,0:T(2,128)S(1)} all-reduce(f32[2,1024]{1,0:T(2,128)S(1)} %pad_maximum_fusion.3), channel_id=1, replica_groups=mesh['groups'=2,'ctx'=16] {'ctx'}, use_global_device_ids=true, to_apply=%region_44.0 | all-reduce | flops 2048 | bytes 16384 | tf_op jit(solution)/shard_map/psum | solution.py:131
  226.7 63.6 %reduce-scatter.7.cloned.1.call-done = f32[64,1024]{1,0:T(8,128)} async-done(((f32[1024,1024]{1,0:T(8,128)}), f32[64,1024]{1,0:T(8,128)}) %reduce-scatter.7.cloned.1.call-update) | async-done | bytes 262160
  292.4 106.1 %reduce-scatter.5.cloned.1.call-done = f32[128,1024]{1,0:T(8,128)} async-done(((f32[2048,1024]{1,0:T(8,128)}), f32[128,1024]{1,0:T(8,128)}) %reduce-scatter.5.cloned.1.call-update) | async-done | bytes 524304 | tf_op jit(solution)/shard_map/reduce_scatter | solution.py:117
  398.5 1.9 broadcast_multiply_fusion.1
  (90 shorter events, 26.7 us)
Async XLA Ops:
  7.2 9.6 %copy-start.14 = (bf16[1024,31]{0,1:T(8,128)(2,1)S(1)}, bf16[1024,31]{0,1:T(8,128)(2,1)}, u32[]{:S(2)}) copy-start(bf16[1024,31]{0,1:T(8,128)(2,1)} %param.13) | copy-start | bytes 190468
  7.2 63.4 %all-gather.3.cloned.1.call-start = ((), (), s32[]{:S(2)}) async-start(), calls=%async_computation.4 | async-start | bytes 4456448 | tf_op jit(solution)/shard_map/all_gather | solution.py:77
  7.9 34.5 %copy-start.15 = (f32[1024]{0:T(1024)S(1)}, f32[1024]{0:T(1024)}, u32[]{:S(2)}) copy-start(f32[1024]{0:T(1024)} %param.11) | copy-start | bytes 12292
  7.9 33.7 %all-to-all-start = ((bf16[16,24,1024]{2,1,0:T(8,128)(2,1)}), bf16[16,24,1024]{2,1,0:T(8,128)(2,1)S(1)}, u32[]{:S(2)}, u32[]{:S(2)}) async-start(bf16[16,24,1024]{2,1,0:T(8,128)(2,1)} %param.8), calls=%async_computation | async-start | bytes 1572864 | tf_op jit(solution)/shard_map/all_to_all | solution.py:65
  15.3 97.4 %all-gather.5.cloned.1.call-start = ((), (), s32[]{:S(2)}) async-start(), calls=%async_computation.5 | async-start | bytes 2228224 | tf_op jit(solution)/shard_map/all_gather | solution.py:88
  16.1 207.2 %all-reduce.2.cloned.1.call-start = ((), (), s32[]{:S(2)}) async-start(), calls=%async_computation.7 | async-start | bytes 262144 | tf_op jit(solution)/shard_map/psum | solution.py:131
  42.7 31.9 %copy-start.7 = (bf16[384,1024]{1,0:T(8,128)(2,1)}, bf16[384,1024]{1,0:T(8,128)(2,1)S(1)}, u32[]{:S(2)}) copy-start(bf16[384,1024]{1,0:T(8,128)(2,1)S(1)} %fusion.72) | copy-start | bytes 2359300
  74.6 1.7 copy-start
  76.3 3.5 collective-permute-start
  78.4 3.1 collective-permute-start.1
  89.0 37.9 %copy-start.4 = (f32[384,1024]{1,0:T(8,128)}, f32[384,1024]{1,0:T(8,128)S(1)}, u32[]{:S(2)}) copy-start(f32[384,1024]{1,0:T(8,128)S(1)} %get-tuple-element.65) | copy-start | bytes 4718596
  89.0 23.7 %copy-start.17 = (f32[1024]{0:T(1024)S(1)}, f32[1024]{0:T(1024)}, u32[]{:S(2)}) copy-start(f32[1024]{0:T(1024)} %param.14) | copy-start | bytes 12292
  121.3 2.7 copy-start.6
  126.7 163.7 %reduce-scatter.7.cloned.1.call-start = ((), (), s32[]{:S(2)}) async-start(), calls=%async_computation.8 | async-start | bytes 4456448
  136.9 7.7 %copy-start.1 = (f32[384,2048]{1,0:T(8,128)S(1)}, f32[384,2048]{1,0:T(8,128)}, u32[]{:S(2)}) copy-start(f32[384,2048]{1,0:T(8,128)} %copy-done) | copy-start | bytes 9437188
  136.9 261.6 %reduce-scatter.5.cloned.1.call-start = ((), (), s32[]{:S(2)}) async-start(), calls=%async_computation.6 | async-start | bytes 8912896 | tf_op jit(solution)/shard_map/reduce_scatter | solution.py:117
  137.9 3.5 collective-permute-start.2
  140.1 3.1 collective-permute-start.3
  158.5 1.6 copy-start.12
  160.1 4.4 %copy-start.13 = (bf16[384,1024]{1,0:T(8,128)(2,1)S(1)}, bf16[384,1024]{1,0:T(8,128)(2,1)}, u32[]{:S(2)}) copy-start(bf16[384,1024]{1,0:T(8,128)(2,1)} %param.9) | copy-start | bytes 2359300
  172.1 8.8 %copy-start.5 = (f32[384,1024]{1,0:T(8,128)S(1)}, f32[384,1024]{1,0:T(8,128)}, u32[]{:S(2)}) copy-start(f32[384,1024]{1,0:T(8,128)} %copy-done.4) | copy-start | bytes 4718596
  172.2 8.8 %copy-start.18 = (f32[1024]{0:T(1024)S(1)}, f32[1024]{0:T(1024)}, u32[]{:S(2)}) copy-start(f32[1024]{0:T(1024)} %param.14) | copy-start | bytes 12292
  173.5 51.3 %all-to-all-start.1 = ((bf16[16,2,12288]{2,1,0:T(2,128)(2,1)}), bf16[16,2,12288]{2,1,0:T(2,128)(2,1)S(1)}, u32[]{:S(2)}, u32[]{:S(2)}) async-start(bf16[16,2,12288]{2,1,0:T(2,128)(2,1)} %reshape.139), calls=%async_computation.1 | async-start | bytes 1572864 | tf_op jit(solution)/shard_map/all_to_all | solution.py:137
  181.0 3.7 copy-start.16
  (6 other events, 6.9 us)
Sparse Core Ops, SparseCore 0:
  10.2 60.3 all-gather.2
  72.7 39.9 all-gather.4
  126.8 86.4 all-reduce.1
  217.0 73.3 reduce-scatter.6
  294.8 103.6 reduce-scatter.4
where the time goes:
time: 408 us; the launch traced here: 407 us
  waiting for transfers between devices  251 us (62%)
  blocking collectives  37.9 us (9%)
  other arithmetic  34.9 us (9%)
  matrix products  26.4 us (6%)
  starting transfers between devices  22.1 us (5%)
  local copies, waits for them, and re-layouts  20.1 us (5%)
  between operations  14.9 us (4%)
    reduce_scatter x1, waiting for transfers between devices, shards(): lax.psum_scatter(frame_sum(grad_projected, scaled_in), 'ctx', scatter_dim...  106 us
    unnamed x6, waiting for transfers between devices  65.1 us
    psum x1, blocking collectives, shards(): depth_total, gains_total = lax.psum((depth_local, gains_local), 'ctx')  37.9 us
    all_gather x1, waiting for transfers between devices, shards(): lax.all_gather(w_in, 'ctx', axis=0, tiled=True)  27.8 us
    all_to_all x1, waiting for transfers between devices, shards(): lax.all_to_all(frames, 'ctx', split_axis=0, concat_axis=1, tiled=True)  24.8 us
    all_gather x1, waiting for transfers between devices, shards(): lax.all_gather(w_out, 'ctx', axis=0, tiled=True)  23.3 us
    unnamed x45, local copies, waits for them, and re-layouts  15 us
    dot_general x2, matrix products, frame_sum(): lax.dot_general(left, right, (((0,), (0,)), ((), ())), preferred_element_...  10.2 us
  transfers between devices with their start and end apart: 11, of which 7 were waited for; matrix products, arithmetic and copies ran while one was open for 15% of the time, Pallas kernels for 0%

commit v1 on v0

--- a/solution.py
+++ b/solution.py
@@ -1,7 +1,13 @@
+import functools
+
 import jax
 import jax.numpy as jnp
 from jax import lax
+from jax.experimental import pallas as pl
+from jax.experimental.pallas import tpu as pltpu
 from jax.sharding import PartitionSpec as P
+
+MESH = pl.DeviceIdType.MESH
 
 epsilon = 1e-05
 
@@ -58,6 +64,167 @@
         begin = taps - 1 - offset
         total = total + padded[begin : begin + length] * kernel[:, offset]
     return total
+
+
+def grid_of(chips):
+    columns = 2 ** ((chips.bit_length() - 1) // 2)
+    return (chips // columns, columns)
+
+
+def chip_at(place, chips):
+    rows, columns = grid_of(chips)
+    inner = columns - 1
+    step = jnp.maximum(place - 1, 0)
+    row = lax.div(step, inner)
+    column = lax.rem(step, inner)
+    column = jnp.where(lax.rem(row, 2) == 0, column, inner - 1 - column)
+    snake = row * columns + 1 + column
+    back = lax.rem(chips - place, chips) * columns
+    return jnp.where((place >= 1) & (place <= rows * inner), snake, back)
+
+
+def place_of(chip, chips):
+    rows, columns = grid_of(chips)
+    inner = columns - 1
+    row = lax.div(chip, columns)
+    column = lax.rem(chip, columns) - 1
+    turned = jnp.where(lax.rem(row, 2) == 0, column, inner - 1 - column)
+    return jnp.where(column < 0, lax.rem(chips - row, chips), row * inner + turned + 1)
+
+
+def position(chips):
+    me = lax.axis_index("ctx")
+    core = lax.rem(me, 2)
+    place = place_of(lax.div(me, 2), chips)
+    right = chip_at(lax.rem(place + 1, chips), chips) * 2 + core
+    left = chip_at(lax.rem(place + chips - 1, chips), chips) * 2 + core
+    return (place, core, me + 1 - 2 * core, right, left)
+
+
+def greet(devices):
+    barrier = pltpu.get_barrier_semaphore()
+    for device in devices:
+        pl.semaphore_signal(barrier, inc=1, device_id={"ctx": device}, device_id_type=MESH)
+    pl.semaphore_wait(barrier, len(devices))
+
+
+def reduce_kernel(
+    chips, first_ref, second_ref, first_out, second_out, outgoing, incoming, held, *sems
+):
+    swap_send, swap_recv, ring_send, ring_recv = sems
+    place, core, partner, right, left = position(chips)
+    upper = first_ref.shape[2]
+    rows = upper + second_ref.shape[2]
+    half = first_ref.shape[3] // 2
+    parts = ((first_ref, first_out, 0, upper), (second_ref, second_out, upper, rows))
+    greet((partner, right, left))
+
+    def owner(way, step):
+        ahead = place + 1 + step if way else place + 2 * chips - 1 - step
+        return chip_at(lax.rem(ahead, chips), chips)
+
+    def swap(step):
+        return pltpu.make_async_remote_copy(
+            src_ref=outgoing.at[step],
+            dst_ref=incoming.at[step],
+            send_sem=swap_send.at[step],
+            recv_sem=swap_recv.at[step],
+            device_id={"ctx": partner},
+            device_id_type=MESH,
+        )
+
+    def hop(way, step):
+        return pltpu.make_async_remote_copy(
+            src_ref=held.at[way, step],
+            dst_ref=held.at[way, step + 1],
+            send_sem=ring_send.at[way, step],
+            recv_sem=ring_recv.at[way, step],
+            device_id={"ctx": left if way else right},
+            device_id_type=MESH,
+        )
+
+    def give(step, carry):
+        for way in range(2):
+            columns = slice(way * half, (way + 1) * half)
+            chip = owner(way, step)
+            for source, _, begin, end in parts:
+                outgoing[step, begin:end, columns] = source[chip, 1 - core, :, columns]
+        swap(step).start()
+        return carry
+
+    def total(way, step, part, arrived):
+        source, _, begin, end = part
+        columns = slice(way * half, (way + 1) * half)
+        value = source[owner(way, step), core, :, columns].astype(jnp.float32)
+        value = value + incoming[step, begin:end, columns].astype(jnp.float32)
+        if arrived:
+            value = value + held[way, step, begin:end, :].astype(jnp.float32)
+        return value
+
+    def move(step, arrived):
+        swap(step).wait_recv()
+        for way in range(2):
+            if arrived:
+                hop(way, step - 1).wait_recv()
+            for part in parts:
+                held[way, step, part[2] : part[3], :] = total(way, step, part, arrived).astype(
+                    held.dtype
+                )
+            hop(way, step).start()
+
+    lax.fori_loop(0, chips, give, 0)
+    move(0, False)
+
+    def middle(step, carry):
+        move(step, True)
+        return carry
+
+    lax.fori_loop(1, chips - 1, middle, 0)
+    swap(chips - 1).wait_recv()
+    for way in range(2):
+        hop(way, chips - 2).wait_recv()
+        for part in parts:
+            part[1][:, way * half : (way + 1) * half] = total(way, chips - 1, part, True)
+
+    def drain(step, carry):
+        swap(step).wait_send()
+        for way in range(2):
+            hop(way, step).wait_send()
+        return carry
+
+    lax.fori_loop(0, chips - 1, drain, 0)
+    swap(chips - 1).wait_send()
+
+
+def reduce_rows(first, second, span):
+    chips = span // 2
+    width = first.shape[1]
+    upper, lower = first.shape[0] // span, second.shape[0] // span
+    rows = upper + lower
+    whole = pl.BlockSpec(memory_space=pltpu.VMEM)
+    return pl.pallas_call(
+        functools.partial(reduce_kernel, chips),
+        out_shape=(
+            jax.ShapeDtypeStruct((upper, width), jnp.float32),
+            jax.ShapeDtypeStruct((lower, width), jnp.float32),
+        ),
+        in_specs=[whole] * 2,
+        out_specs=(whole,) * 2,
+        scratch_shapes=[
+            pltpu.VMEM((chips, rows, width), first.dtype),
+            pltpu.VMEM((chips, rows, width), first.dtype),
+            pltpu.VMEM((2, chips, rows, width // 2), first.dtype),
+            pltpu.SemaphoreType.DMA((chips,)),
+            pltpu.SemaphoreType.DMA((chips,)),
+            pltpu.SemaphoreType.DMA((2, chips - 1)),
+            pltpu.SemaphoreType.DMA((2, chips - 1)),
+        ],
+        compiler_params=pltpu.CompilerParams(
+            collective_id=0, has_side_effects=True, vmem_limit_bytes=44 * 2**20
+        ),
+        cost_estimate=pl.CostEstimate(flops=10**7, bytes_accessed=120 * 10**6, transcendentals=0),
+        name="reduce_rows",
+    )(first.reshape(chips, 2, upper, width), second.reshape(chips, 2, lower, width))
 
 
 def shards(frames, grad_out, valid_count, norm_gain, w_in, depth_weight, depth_gain, w_out):
@@ -87,9 +254,8 @@
     act = (gained * sig_two * keep).astype(jnp.bfloat16)
     mixed = times_transposed(act, lax.all_gather(w_out, "ctx", axis=0, tiled=True))
     output = (wide_in + mixed).astype(jnp.bfloat16)
-    grad_w_out = (
-        lax.psum_scatter(frame_sum(grad_out, act), "ctx", scatter_dimension=0, tiled=True) * scale
-    )
+    sent = jnp.bfloat16 if span <= 32 else jnp.float32
+    partial_out = frame_sum(grad_out, act).astype(sent)
     columns = grad_out
     grad_act = jnp.dot(
         columns,
@@ -108,17 +274,15 @@
             jnp.sum(grad_wide * padded[offset : offset + local_frames], axis=0)
             for offset in range(taps)
         ],
-        axis=1,
+        axis=0,
     )
     grad_projected = jnp.concatenate(
         [grad_glu * sigma, grad_glu * linear * sigma * (1.0 - sigma)], axis=1
     ).astype(jnp.bfloat16)
-    grad_w_in = (
-        lax.psum_scatter(
-            frame_sum(grad_projected, scaled_in), "ctx", scatter_dimension=0, tiled=True
-        )
-        * scale
-    )
+    partial_in = frame_sum(grad_projected, scaled_in).astype(sent)
+    rows_in, rows_out = reduce_rows(partial_in, partial_out, span)
+    grad_w_in = rows_in * scale
+    grad_w_out = rows_out * scale
     columns = grad_projected
     grad_scaled = jnp.dot(
         columns, lax.all_gather(w_in, "ctx", axis=0, tiled=True), preferred_element_type=jnp.float32
@@ -128,7 +292,11 @@
         [jnp.sum(grad_scaled * normed_in, axis=0), jnp.sum(grad_gained * normed_conv, axis=0)],
         axis=0,
     )
-    depth_total, gains_total = lax.psum((depth_local, gains_local), "ctx")
+    blank = jnp.zeros((-(taps + 2) % 16, width), jnp.float32)
+    small = jnp.concatenate([depth_local, gains_local, blank], axis=0)
+    small = lax.psum_scatter(small.reshape(-1, 128), "ctx", scatter_dimension=0, tiled=True)
+    small = lax.all_gather(small, "ctx", axis=0, tiled=True).reshape(-1, width)
+    depth_total, gains_total = small[:taps].T, small[taps : taps + 2]
     grad_local = (
         (grad_out.astype(jnp.float32) + grad_in)
         .astype(jnp.bfloat16)

time: 408 us -> 254 us (0.62)
  waiting for transfers between devices: 251 us -> 78.6 us
  Pallas kernels: 0 us -> 50 us
  blocking collectives: 37.9 us -> 24.3 us
  local copies, waits for them, and re-layouts: 20.1 us -> 12.2 us
  matrix products: 26.4 us -> 19.9 us
    reduce_scatter x1 -> x0, waiting for transfers between devices: 106 us -> none  [shards(): lax.psum_scatter(frame_sum(grad_projected, scaled_in), 'ctx', scatter_dim...]
    unnamed x6 -> x4, waiting for transfers between devices: 65.1 us -> 1.95 us
    pallas_call x0 -> x1, Pallas kernels: none -> 50 us  [reduce_rows(): pl.pallas_call(functools.partial(reduce_kernel, chips), out_shape=(jax.Sh...]
    psum x1 -> x0, blocking collectives: 37.9 us -> none  [shards(): depth_total, gains_total = lax.psum((depth_local, gains_local), 'ctx')]
    all_gather x0 -> x1, blocking collectives: none -> 24.3 us  [shards(): small = lax.all_gather(small, 'ctx', axis=0, tiled=True).reshape(-1, width)]
    unnamed x45 -> x36, local copies, waits for them, and re-layouts: 15 us -> 8.29 us
  transfers between devices with their start and end apart: 11 -> 9, of which waited for: 7 -> 5; matrix products, arithmetic and copies ran while one was open for 15% -> 11% of each run, Pallas kernels for 0% -> 20%
where the time goes in v1:
time: 254 us; the launch traced here: 253 us
  waiting for transfers between devices  78.6 us (31%)
  Pallas kernels  50 us (20%)
  other arithmetic  31.5 us (12%)
  blocking collectives  24.3 us (10%)
  starting transfers between devices  21.7 us (9%)
  matrix products  19.9 us (8%)
  between operations  14.9 us (6%)
  local copies, waits for them, and re-layouts  12.2 us (5%)
    pallas_call x1, Pallas kernels, reduce_rows(): pl.pallas_call(functools.partial(reduce_kernel, chips), out_shape=(jax.Sh...  50 us
    all_gather x1, waiting for transfers between devices, shards(): lax.all_gather(w_in, 'ctx', axis=0, tiled=True)  27.9 us
    all_to_all x1, waiting for transfers between devices, shards(): lax.all_to_all(frames, 'ctx', split_axis=0, concat_axis=1, tiled=True)  24.8 us
    all_gather x1, blocking collectives, shards(): small = lax.all_gather(small, 'ctx', axis=0, tiled=True).reshape(-1, width)  24.3 us
    all_gather x1, waiting for transfers between devices, shards(): lax.all_gather(w_out, 'ctx', axis=0, tiled=True)  22.2 us
    unnamed x36, local copies, waits for them, and re-layouts  8.29 us
    another operation x2, other arithmetic  7.57 us
    reduce_sum x2, other arithmetic, normalize(): center = jnp.mean(values, axis=-1, keepdims=True)  7.41 us
  transfers between devices with their start and end apart: 9, of which 5 were waited for; matrix products, arithmetic and copies ran while one was open for 11% of the time, Pallas kernels for 20%

profile of v1, /device:TPU:0, one launch (start us, length us, event | category | flops | bytes accessed | tf_op | source)
XLA Modules:
  0.0 253.1 jit_solution(6229267633196334438)
XLA Ops:
  7.9 7.4 %all-to-all-start = ((bf16[16,24,1024]{2,1,0:T(8,128)(2,1)}), bf16[16,24,1024]{2,1,0:T(8,128)(2,1)S(1)}, u32[]{:S(2)}, u32[]{:S(2)}) async-start(bf16[16,24,1024]{2,1,0:T(8,128)(2,1)} %param.8), calls=%async_computation | async-start | bytes 1572864 | tf_op jit(solution)/shard_map/all_to_all | solution.py:232
  16.8 24.8 %all-to-all-done = bf16[16,24,1024]{2,1,0:T(8,128)(2,1)S(1)} async-done(((bf16[16,24,1024]{2,1,0:T(8,128)(2,1)}), bf16[16,24,1024]{2,1,0:T(8,128)(2,1)S(1)}, u32[]{:S(2)}, u32[]{:S(2)}) %all-to-all-start) | async-done | bytes 786464 | tf_op jit(solution)/shard_map/all_to_all | solution.py:232
  42.7 27.9 %all-gather.3.cloned.1.call-done = bf16[2048,1024]{1,0:T(8,128)(2,1)} async-done(((bf16[128,1024]{1,0:T(8,128)(2,1)}), bf16[2048,1024]{1,0:T(8,128)(2,1)}) %all-gather.3.cloned.1.call-update) | async-done | bytes 4194320 | tf_op jit(solution)/shard_map/all_gather | solution.py:244
  70.6 4.0 %fusion.90 = f32[384,2048]{1,0:T(8,128)S(1)} fusion(bf16[384,1024]{1,0:T(8,128)(2,1)S(1)} %fusion.72, bf16[2048,1024]{1,0:T(8,128)(2,1)} %all-gather.3.cloned.1.call-done), kind=kOutput, calls=%fused_computation.189 | convolution fusion | flops 1610612736 | bytes 8126464 | tf_op jit(solution)/shard_map/dot_general | solution.py:48
  76.3 2.2 collective-permute-start
  78.4 1.3 collective-permute-start.1
  79.8 1.7 collective-permute-done.1
  81.8 7.2 %fusion.85 = (f32[384]{0:T(512)S(1)}, f32[384,1024]{1,0:T(8,128)S(1)}) fusion(f32[1024]{0:T(1024)S(1)} %bitcast.182, f32[414,1024]{1,0:T(8,128)S(1)} %maximum_convert_fusion, f32[1024]{0:T(1024)S(1)} %bitcast.180, f32[1024]{0:T(1024)S(1)} %bitcast.178, f32[1024]{0:T(1024)S(1)} %bitcast.176, f32[1024]{0:T(1024)S(1)} %bitcast.174, f32[1024]{0:T(1024)S(1)} %bitcast.172, ...), kind=kLoop, calls=%fused_computation.183 | loop fusion | flops 24379008 | bytes 50460160 | tf_op jit(solution)/shard_map/reduce_sum | solution.py:29
  90.5 22.2 %all-gather.5.cloned.1.call-done = bf16[1024,1024]{1,0:T(8,128)(2,1)} async-done(((bf16[64,1024]{1,0:T(8,128)(2,1)}), bf16[1024,1024]{1,0:T(8,128)(2,1)}) %all-gather.5.cloned.1.call-update) | async-done | bytes 2097168 | tf_op jit(solution)/shard_map/all_gather | solution.py:255
  112.7 4.4 %multiply_reduce_fusion = (f32[1024]{0:T(1024)}, f32[384]{0:T(512)S(1)}, f32[384]{0:T(512)S(1)}, f32[384,1024]{1,0:T(8,128)S(1)}) fusion(f32[384,1024]{1,0:T(8,128)} %copy-done.2, f32[384]{0:T(512)S(1)} %add_rsqrt_fusion.1, f32[384]{0:T(512)S(1)} %broadcast_multiply_fusion.7, f32[1024]{0:T(1024)S(1)} %copy-done.11, f32[384]{0:T(512)S(1)} %fusion.81, ...), kind=kOutput, calls=%fused_computation.150 | convolution fusion | flops 812382464 | bytes 6045184 | tf_op jit(solution)/shard_map/dot_general | solution.py:260
  117.1 4.5 %fusion.30 = (f32[1024]{0:T(1024)S(1)}, f32[1024]{0:T(1024)S(1)}, f32[1024]{0:T(1024)S(1)}, f32[1024]{0:T(1024)S(1)}, f32[1024]{0:T(1024)S(1)}, /*index=5*/f32[1...) fusion(f32[414,1024]{1,0:T(8,128)S(1)} %maximum_convert_fusion,, ...), kind=kLoop, calls=%fused_computation.63 | loop fusion | flops 17676288 | bytes 32327680 | tf_op jit(solution)/shard_map/reduce_sum | solution.py:274
  121.7 2.6 %fusion.29 = (f32[1024]{0:T(1024)S(1)}, f32[1024]{0:T(1024)S(1)}, f32[1024]{0:T(1024)S(1)}, f32[1024]{0:T(1024)S(1)}, f32[1024]{0:T(1024)S(1)}, /*index=5*/f32[1...) fusion(bf16[384,1024]{1,0:T(8,128)(2,1)S(1)} %get-tuple-element, ...), kind=kLoop, calls=%fused_computation.62 | loop fusion | flops 10603520 | bytes 21286912 | tf_op jit(solution)/shard_map/reduce_sum | solution.py:274
  124.3 2.2 collective-permute-start.2
  127.8 2.1 fusion.79
  130.2 6.9 %multiply_convert_fusion.1 = (bf16[384,1024]{1,0:T(8,128)(2,1)S(1)}, f32[384,1024]{1,0:T(8,128)S(1)}) fusion(f32[384,2048]{1,0:T(8,128)S(1)} %copy-done.1, f32[384]{0:T(512)S(1)} %fusion.81, f32[1024]{0:T(1024)S(1)} %bitcast.183, f32[414,1024]{1,0:T(8,128)S(1)} %maximum_convert_fusion.1, f32[1024]{0:T(1024)S(1)} %bitcast.181, f32[1024]{0:T(1024)S(1)} %bitcast.179, ...), kind=kLoop, calls=%fused_computation.152 | loop fusion | flops 26345472 | bytes 52819456 | tf_op jit(solution)/shard_map/convert.1
  138.1 1.8 copy-done.14
  139.9 2.2 fusion.78
  144.5 5.2 %reduce.8 = bf16[384,1024]{1,0:T(8,128)(2,1)S(1)} reduce(bf16[384,1,1024]{2,1,0:T(2,128)(2,1)S(1)} %bitcast.117, bf16[]{:T(256)} %broadcast.124), dimensions={1}, to_apply=%bitcast.113.reduce_sub_computation | reduce | bytes 1572866
  149.8 1.4 reshape.157
  151.1 7.1 %all-to-all-start.1 = ((bf16[16,2,12288]{2,1,0:T(2,128)(2,1)}), bf16[16,2,12288]{2,1,0:T(2,128)(2,1)S(1)}, u32[]{:S(2)}, u32[]{:S(2)}) async-start(bf16[16,2,12288]{2,1,0:T(2,128)(2,1)} %reshape.157), calls=%async_computation.1 | async-start | bytes 1572864 | tf_op jit(solution)/shard_map/all_to_all | solution.py:305
  158.5 3.2 %convolution_convert_fusion.1 = bf16[1024,1024]{0,1:T(8,128)(2,1)S(1)} fusion(bf16[384,1024]{1,0:T(8,128)(2,1)} %param.9, f32[384,1024]{1,0:T(8,128)} %copy-done.2, f32[1024]{0:T(1024)S(1)} %copy-done.13, f32[384]{0:T(512)S(1)} %add_rsqrt_fusion.1, f32[384]{0:T(512)S(1)} %broadcast_multiply_fusion.7, f32[384]{0:T(512)S(1)} %fusion.81), kind=kOutput, calls=%fused_computation.32 | convolution fusion | flops 809893888 | bytes 4465152 | tf_op jit(solution)/shard_map/dot_general | solution.py:42
  162.9 4.0 %convolution_convert_fusion = bf16[2048,1024]{1,0:T(8,128)(2,1)S(1)} fusion(bf16[384,1024]{1,0:T(8,128)(2,1)} %copy-done.4, bf16[384,1024]{1,0:T(8,128)(2,1)} %copy-done.6, bf16[384,1024]{1,0:T(8,128)(2,1)} %copy-done.7), kind=kOutput, calls=%fused_computation.31 | convolution fusion | flops 1615855616 | bytes 6553600 | tf_op jit(solution)/shard_map/dot_general | solution.py:42
  166.9 50.0 %reduce_rows.1 = (f32[128,1024]{1,0:T(8,128)S(1)}, f32[64,1024]{1,0:T(8,128)S(1)}) custom-call(bf16[8,2,128,1024]{3,2,1,0:T(8,128)(2,1)S(1)} %bitcast.115, bf16[8,2,64,1024]{3,2,1,0:T(8,128)(2,1)S(1)} %bitcast.116), custom_call_target="tpu_custom_call" | custom-call | flops 10000000 | bytes 120000000 | tf_op jit(solution)/shard_map/reduce_rows/pallas_call | solution.py:205
  219.1 24.3 %all_gather.13 = f32[384,128]{1,0:T(8,128)S(1)} all-gather(f32[24,128]{1,0:T(8,128)} %reduce-scatter.4.cloned.1.call-done), channel_id=1, replica_groups=mesh['groups'=2,'ctx'=16] {'ctx'}, dimensions={0}, use_global_device_ids=true | all-gather | bytes 208896 | tf_op jit(solution)/shard_map/all_gather | solution.py:298
  (79 shorter events, 17.6 us)
Async XLA Ops:
  7.2 9.6 %copy-start.8 = (bf16[1024,31]{0,1:T(8,128)(2,1)S(1)}, bf16[1024,31]{0,1:T(8,128)(2,1)}, u32[]{:S(2)}) copy-start(bf16[1024,31]{0,1:T(8,128)(2,1)} %param.13) | copy-start | bytes 190468
  7.2 63.4 %all-gather.3.cloned.1.call-start = ((), (), s32[]{:S(2)}) async-start(), calls=%async_computation.3 | async-start | bytes 4456448 | tf_op jit(solution)/shard_map/all_gather | solution.py:244
  7.9 34.5 %copy-start.9 = (f32[1024]{0:T(1024)S(1)}, f32[1024]{0:T(1024)}, u32[]{:S(2)}) copy-start(f32[1024]{0:T(1024)} %param.11) | copy-start | bytes 12292
  7.9 33.7 %all-to-all-start = ((bf16[16,24,1024]{2,1,0:T(8,128)(2,1)}), bf16[16,24,1024]{2,1,0:T(8,128)(2,1)S(1)}, u32[]{:S(2)}, u32[]{:S(2)}) async-start(bf16[16,24,1024]{2,1,0:T(8,128)(2,1)} %param.8), calls=%async_computation | async-start | bytes 1572864 | tf_op jit(solution)/shard_map/all_to_all | solution.py:232
  15.3 97.4 %all-gather.5.cloned.1.call-start = ((), (), s32[]{:S(2)}) async-start(), calls=%async_computation.4 | async-start | bytes 2228224 | tf_op jit(solution)/shard_map/all_gather | solution.py:255
  42.7 31.9 %copy-start.4 = (bf16[384,1024]{1,0:T(8,128)(2,1)}, bf16[384,1024]{1,0:T(8,128)(2,1)S(1)}, u32[]{:S(2)}) copy-start(bf16[384,1024]{1,0:T(8,128)(2,1)S(1)} %fusion.72) | copy-start | bytes 2359300
  74.6 1.7 copy-start
  76.3 3.5 %collective-permute-start = (bf16[15,1024]{1,0:T(8,128)(2,1)S(1)}, bf16[15,1024]{1,0:T(8,128)(2,1)S(1)}, u32[]{:S(2)}, u32[]{:S(2)}) collective-permute-start(bf16[15,1024]{1,0:T(8,128)(2,1)S(1)} %get-tuple-element.54), channel_id=1, source_target_pairs={{0,1},{1,2},{2,3},{3,4},{4,5},{5,6},{6,7},{7,8},{8,9},{9,10},{10,1... | collective-permute-start | bytes 92168 | tf_op jit(solution)/shard_map/ppermute | solution.py:20
  78.4 3.1 %collective-permute-start.1 = (bf16[15,1024]{1,0:T(8,128)(2,1)S(1)}, bf16[15,1024]{1,0:T(8,128)(2,1)S(1)}, u32[]{:S(2)}, u32[]{:S(2)}) collective-permute-start(bf16[15,1024]{1,0:T(8,128)(2,1)S(1)} %get-tuple-element.55), channel_id=1, source_target_pairs={{1,0},{2,1},{3,2},{4,3},{5,4},{6,5},{7,6},{8,7},{9,8},{10,9},{11,1... | collective-permute-start | bytes 92168 | tf_op jit(solution)/shard_map/ppermute | solution.py:23
  89.0 1.2 copy-start.2
  89.0 23.7 %copy-start.5 = (bf16[384,1024]{1,0:T(8,128)(2,1)S(1)}, bf16[384,1024]{1,0:T(8,128)(2,1)}, u32[]{:S(2)}) copy-start(bf16[384,1024]{1,0:T(8,128)(2,1)} %param.9) | copy-start | bytes 2359300
  89.1 23.6 %copy-start.11 = (f32[1024]{0:T(1024)S(1)}, f32[1024]{0:T(1024)}, u32[]{:S(2)}) copy-start(f32[1024]{0:T(1024)} %param.14) | copy-start | bytes 12292
  112.7 4.4 %copy-start.3 = (f32[384,1024]{1,0:T(8,128)S(1)}, f32[384,1024]{1,0:T(8,128)}, u32[]{:S(2)}) copy-start(f32[384,1024]{1,0:T(8,128)} %copy-done.2) | copy-start | bytes 4718596
  121.7 6.1 %copy-start.12 = (f32[1024]{0:T(1024)S(1)}, f32[1024]{0:T(1024)}, u32[]{:S(2)}) copy-start(f32[1024]{0:T(1024)} %param.14) | copy-start | bytes 12292
  121.7 6.1 %copy-start.15 = (bf16[1024,1024]{1,0:T(8,128)(2,1)S(1)}, bf16[1024,1024]{1,0:T(8,128)(2,1)}, u32[]{:S(2)}) copy-start(bf16[1024,1024]{1,0:T(8,128)(2,1)} %all-gather.5.cloned.1.call-done) | copy-start | bytes 6291460
  124.3 5.6 %collective-permute-start.2 = (bf16[15,1024]{1,0:T(8,128)(2,1)S(1)}, bf16[15,1024]{1,0:T(8,128)(2,1)S(1)}, u32[]{:S(2)}, u32[]{:S(2)}) collective-permute-start(bf16[15,1024]{1,0:T(8,128)(2,1)S(1)} %get-tuple-element.52), channel_id=1, source_target_pairs={{0,1},{1,2},{2,3},{3,4},{4,5},{5,6},{6,7},{7,8},{8,9},{9,10},{10,1... | collective-permute-start | bytes 92168 | tf_op jit(solution)/shard_map/ppermute | solution.py:20
  126.5 3.5 %collective-permute-start.3 = (bf16[15,1024]{1,0:T(8,128)(2,1)S(1)}, bf16[15,1024]{1,0:T(8,128)(2,1)S(1)}, u32[]{:S(2)}, u32[]{:S(2)}) collective-permute-start(bf16[15,1024]{1,0:T(8,128)(2,1)S(1)} %get-tuple-element.53), channel_id=1, source_target_pairs={{1,0},{2,1},{3,2},{4,3},{5,4},{6,5},{7,6},{8,7},{9,8},{10,9},{11,1... | collective-permute-start | bytes 92168 | tf_op jit(solution)/shard_map/ppermute | solution.py:23
  127.8 2.4 copy-start.1
  137.1 2.8 %copy-start.14 = (bf16[2048,1024]{1,0:T(8,128)(2,1)S(1)}, bf16[2048,1024]{1,0:T(8,128)(2,1)}, u32[]{:S(2)}) copy-start(bf16[2048,1024]{1,0:T(8,128)(2,1)} %all-gather.3.cloned.1.call-done) | copy-start | bytes 12582916
  137.8 4.2 %copy-start.6 = (bf16[384,1024]{1,0:T(8,128)(2,1)}, bf16[384,1024]{1,0:T(8,128)(2,1)S(1)}, u32[]{:S(2)}) copy-start(bf16[384,1024]{1,0:T(8,128)(2,1)S(1)} %multiply_convert_fusion) | copy-start | bytes 2359300
  149.8 8.8 %copy-start.13 = (f32[1024]{0:T(1024)S(1)}, f32[1024]{0:T(1024)}, u32[]{:S(2)}) copy-start(f32[1024]{0:T(1024)} %param.14) | copy-start | bytes 12292
  151.1 93.5 %all-to-all-start.1 = ((bf16[16,2,12288]{2,1,0:T(2,128)(2,1)}), bf16[16,2,12288]{2,1,0:T(2,128)(2,1)S(1)}, u32[]{:S(2)}, u32[]{:S(2)}) async-start(bf16[16,2,12288]{2,1,0:T(2,128)(2,1)} %reshape.157), calls=%async_computation.1 | async-start | bytes 1572864 | tf_op jit(solution)/shard_map/all_to_all | solution.py:305
  158.2 3.5 %copy-start.10 = (f32[1024]{0:T(1024)S(1)}, f32[1024]{0:T(1024)}, u32[]{:S(2)}) copy-start(f32[1024]{0:T(1024)} %get-tuple-element.10) | copy-start | bytes 12292
  158.2 60.8 %reduce-scatter.4.cloned.1.call-start = ((), (), s32[]{:S(2)}) async-start(), calls=%async_computation.5 | async-start | bytes 208896
  (1 other events, 0.9 us)
Sparse Core Ops, SparseCore 0:
  10.2 60.3 all-gather.2
  72.7 39.9 all-gather.4
  163.0 55.9 reduce-scatter.3

commit v2 on v1

--- a/solution.py
+++ b/solution.py
@@ -227,8 +227,125 @@
     )(first.reshape(chips, 2, upper, width), second.reshape(chips, 2, lower, width))
 
 
+def gather_kernel(
+    chips, first_ref, second_ref, first_out, second_out, local, *sems
+):
+    ring_send, ring_recv, swap_send, swap_recv = sems
+    place, core, partner, right, left = position(chips)
+    last = chips // 2 - 1
+    half = first_ref.shape[1] // 2
+    pairs = ((first_ref, first_out), (second_ref, second_out))
+    greet((partner, right, left))
+
+    def block(which, way, step, side, cut):
+        ahead = place + step if way else place + chips - step
+        columns = slice(way * half, (way + 1) * half) if cut else slice(None)
+        return pairs[which][1].at[chip_at(lax.rem(ahead, chips), chips), side, :, columns]
+
+    def send(source, target, send_sem, recv_sem, device):
+        return pltpu.make_async_remote_copy(
+            src_ref=source,
+            dst_ref=target,
+            send_sem=send_sem,
+            recv_sem=recv_sem,
+            device_id={"ctx": device},
+            device_id_type=MESH,
+        )
+
+    def hop(which, way, step, cut, arriving=False, source=None):
+        target = block(which, way, step + 1 if arriving else step, core, cut)
+        return send(
+            target if source is None else source,
+            target,
+            ring_send.at[which, way, step],
+            ring_recv.at[which, way, step],
+            left if way else right,
+        )
+
+    def swap(which, way, step, side, cut, source=None):
+        target = block(which, way, step, side, cut)
+        return send(
+            target if source is None else source,
+            target,
+            swap_send.at[which, way, step],
+            swap_recv.at[which, way, step],
+            partner,
+        )
+
+    def keep(which):
+        return pltpu.make_async_copy(
+            pairs[which][0], block(which, 0, 0, core, False), local.at[which]
+        )
+
+    for which in range(2):
+        for way in range(2):
+            hop(which, way, 0, False, source=pairs[which][0]).start()
+    for which in range(2):
+        swap(which, 0, 0, core, False, source=pairs[which][0]).start()
+        keep(which).start()
+
+    def forward(step, cut):
+        for which in range(2):
+            for way in range(2):
+                hop(which, way, step - 1, False, arriving=True).wait_recv()
+                hop(which, way, step, cut).start()
+                swap(which, way, step, core, False).start()
+
+    def middle(step, carry):
+        forward(step, False)
+        return carry
+
+    lax.fori_loop(1, last, middle, 0)
+    forward(last, True)
+    for which in range(2):
+        for way in range(2):
+            hop(which, way, last, True, arriving=True).wait_recv()
+            swap(which, way, last + 1, core, True).start()
+
+    def drain(step, carry):
+        for which in range(2):
+            for way in range(2):
+                hop(which, way, step, False).wait_send()
+                swap(which, way, step + 1, core, False).wait_send()
+                swap(which, way, step + 1, 1 - core, False).wait_recv()
+        return carry
+
+    lax.fori_loop(0, last, drain, 0)
+    for which in range(2):
+        keep(which).wait()
+        swap(which, 0, 0, core, False, source=pairs[which][0]).wait_send()
+        swap(which, 0, 0, 1 - core, False).wait_recv()
+        for way in range(2):
+            hop(which, way, last, True).wait_send()
+            swap(which, way, last + 1, core, True).wait_send()
+            swap(which, way, last + 1, 1 - core, True).wait_recv()
+
+
+def gather_rows(first, second, span):
+    chips = span // 2
+    width = first.shape[1]
+    kept = pl.BlockSpec(memory_space=pl.ANY)
+    ring = pltpu.SemaphoreType.DMA((2, 2, chips // 2))
+    swaps = pltpu.SemaphoreType.DMA((2, 2, chips // 2 + 1))
+    whole_first, whole_second = pl.pallas_call(
+        functools.partial(gather_kernel, chips),
+        out_shape=(
+            jax.ShapeDtypeStruct((chips, 2) + first.shape, first.dtype),
+            jax.ShapeDtypeStruct((chips, 2) + second.shape, second.dtype),
+        ),
+        in_specs=[kept] * 2,
+        out_specs=(kept,) * 2,
+        scratch_shapes=[pltpu.SemaphoreType.DMA((2,)), ring, ring, swaps, swaps],
+        compiler_params=pltpu.CompilerParams(collective_id=1, has_side_effects=True),
+        cost_estimate=pl.CostEstimate(flops=10**7, bytes_accessed=120 * 10**6, transcendentals=0),
+        name="gather_rows",
+    )(first, second)
+    return (whole_first.reshape(-1, width), whole_second.reshape(-1, width))
+
+
 def shards(frames, grad_out, valid_count, norm_gain, w_in, depth_weight, depth_gain, w_out):
     span = lax.axis_size("ctx")
+    whole_in, whole_out = gather_rows(w_in, w_out, span)
     ordered = lax.all_to_all(frames, "ctx", split_axis=0, concat_axis=1, tiled=True)
     local_frames = ordered.shape[1]
     width = ordered.shape[2]
@@ -241,7 +358,7 @@
     wide_in = inputs.astype(jnp.float32)
     normed_in, inverse_in = normalize(wide_in)
     scaled_in = (normed_in * norm_gain).astype(jnp.bfloat16)
-    projected = times_transposed(scaled_in, lax.all_gather(w_in, "ctx", axis=0, tiled=True))
+    projected = times_transposed(scaled_in, whole_in)
     linear = projected[:, :width]
     sigma = jax.nn.sigmoid(projected[:, width:])
     glu = (linear * sigma * keep).astype(jnp.bfloat16)
@@ -252,14 +369,14 @@
     gained = normed_conv * depth_gain
     sig_two = jax.nn.sigmoid(gained)
     act = (gained * sig_two * keep).astype(jnp.bfloat16)
-    mixed = times_transposed(act, lax.all_gather(w_out, "ctx", axis=0, tiled=True))
+    mixed = times_transposed(act, whole_out)
     output = (wide_in + mixed).astype(jnp.bfloat16)
     sent = jnp.bfloat16 if span <= 32 else jnp.float32
     partial_out = frame_sum(grad_out, act).astype(sent)
     columns = grad_out
     grad_act = jnp.dot(
         columns,
-        lax.all_gather(w_out, "ctx", axis=0, tiled=True),
+        whole_out,
         preferred_element_type=jnp.float32,
     )
     grad_gained = grad_act * keep * (sig_two * (1.0 + gained * (1.0 - sig_two)))
@@ -285,7 +402,7 @@
     grad_w_out = rows_out * scale
     columns = grad_projected
     grad_scaled = jnp.dot(
-        columns, lax.all_gather(w_in, "ctx", axis=0, tiled=True), preferred_element_type=jnp.float32
+        columns, whole_in, preferred_element_type=jnp.float32
     )
     grad_in = norm_backward(grad_scaled * norm_gain, normed_in, inverse_in)
     gains_local = jnp.stack(
@@ -297,12 +414,10 @@
     small = lax.psum_scatter(small.reshape(-1, 128), "ctx", scatter_dimension=0, tiled=True)
     small = lax.all_gather(small, "ctx", axis=0, tiled=True).reshape(-1, width)
     depth_total, gains_total = small[:taps].T, small[taps : taps + 2]
-    grad_local = (
-        (grad_out.astype(jnp.float32) + grad_in)
-        .astype(jnp.bfloat16)
-        .reshape(1, local_frames, width)
-    )
-    grad_frames = lax.all_to_all(grad_local, "ctx", split_axis=1, concat_axis=0, tiled=True)
+    grad_local = (grad_out.astype(jnp.float32) + grad_in).astype(jnp.bfloat16)
+    grad_frames = lax.all_to_all(
+        grad_local.reshape(frames.shape), "ctx", split_axis=0, concat_axis=0, tiled=True
+    )
     return (output, grad_frames, grad_w_in, grad_w_out, depth_total * scale, gains_total * scale)
 
 

time: 254 us -> 221 us (0.87)
  waiting for transfers between devices: 78.6 us -> 2.24 us
  Pallas kernels: 50 us -> 102 us
  local copies, waits for them, and re-layouts: 12.2 us -> 7.96 us
  other arithmetic: 31.5 us -> 28.2 us
    pallas_call x0 -> x1, Pallas kernels: none -> 51.3 us  [gather_rows(): pl.pallas_call(functools.partial(gather_kernel, chips), out_shape=(jax.Sh...]
    all_gather x2 -> x0, waiting for transfers between devices: 50 us -> none  [the longest x1 27.9 us: shards(): lax.all_gather(w_in, 'ctx', axis=0, tiled=True)]
    all_to_all x1, waiting for transfers between devices: 24.8 us -> 0.01 us  [shards(): lax.all_to_all(frames, 'ctx', split_axis=0, concat_axis=1, tiled=True)]
    unnamed x1 -> x0, other arithmetic: 5.24 us -> none
    unnamed x36 -> x25, local copies, waits for them, and re-layouts: 8.29 us -> 5.26 us
  transfers between devices with their start and end apart: 9 -> 7, of which waited for: 5 -> 1; matrix products, arithmetic and copies ran while one was open for 11% -> 6% of each run, Pallas kernels for 20% -> 46%
where the time goes in v2:
time: 221 us
  Pallas kernels  102 us (46%)
  other arithmetic  28.2 us (13%)
  blocking collectives  24.1 us (11%)
  starting transfers between devices  23.1 us (10%)
  matrix products  18 us (8%)
  between operations  15.1 us (7%)
  local copies, waits for them, and re-layouts  7.96 us (4%)
  waiting for transfers between devices  2.24 us (1%)
    pallas_call x1, Pallas kernels, gather_rows(): pl.pallas_call(functools.partial(gather_kernel, chips), out_shape=(jax.Sh...  51.3 us
    pallas_call x1, Pallas kernels, reduce_rows(): pl.pallas_call(functools.partial(reduce_kernel, chips), out_shape=(jax.Sh...  50.6 us
    all_gather x1, blocking collectives, shards(): small = lax.all_gather(small, 'ctx', axis=0, tiled=True).reshape(-1, width)  24.1 us
    all_to_all x1, starting transfers between devices, shards(): lax.all_to_all(frames, 'ctx', split_axis=0, concat_axis=1, tiled=True)  7.53 us
    reduce_sum x2, other arithmetic, normalize(): center = jnp.mean(values, axis=-1, keepdims=True)  7.41 us
    another operation x2, other arithmetic  7.37 us
    reduce_sum x2, other arithmetic, shards(): jnp.sum(grad_wide * padded[offset:offset + local_frames], axis=0)  7.26 us
    dot_general x2, matrix products, frame_sum(): lax.dot_general(left, right, (((0,), (0,)), ((), ())), preferred_element_...  7.19 us
  transfers between devices with their start and end apart: 7, of which 1 were waited for; matrix products, arithmetic and copies ran while one was open for 6% of the time, Pallas kernels for 46%

profile of v2, /device:TPU:0, one launch (start us, length us, event | category | flops | bytes accessed | tf_op | source)
XLA Modules:
  0.0 220.5 jit_solution(17626842352289877210)
XLA Ops:
  7.2 7.5 %all-to-all-start = ((bf16[16,24,1024]{2,1,0:T(8,128)(2,1)}), bf16[16,24,1024]{2,1,0:T(8,128)(2,1)S(1)}, u32[]{:S(2)}, u32[]{:S(2)}) async-start(bf16[16,24,1024]{2,1,0:T(8,128)(2,1)} %param.8), calls=%async_computation | async-start | bytes 1572864 | tf_op jit(solution)/shard_map/all_to_all | solution.py:349
  15.4 51.3 %gather_rows.1 = (bf16[8,2,128,1024]{3,2,1,0:T(8,128)(2,1)}, bf16[8,2,64,1024]{3,2,1,0:T(8,128)(2,1)}) custom-call(bf16[128,1024]{1,0:T(8,128)(2,1)} %first_ref.1, bf16[64,1024]{1,0:T(8,128)(2,1)} %second_ref.1), custom_call_target="tpu_custom_call" | custom-call | flops 10000000 | bytes 120000000 | tf_op jit(solution)/shard_map/gather_rows/pallas_call | solution.py:330
  67.7 4.0 %fusion.93 = f32[384,2048]{1,0:T(8,128)S(1)} fusion(bf16[384,1024]{1,0:T(8,128)(2,1)S(1)} %bitcast.117, bf16[2048,1024]{1,0:T(8,128)(2,1)} %bitcast.214), kind=kOutput, calls=%fused_computation.191 | convolution fusion | flops 1610612736 | bytes 8126464 | tf_op jit(solution)/shard_map/dot_general | solution.py:48
  73.0 2.3 %collective-permute-start = (bf16[15,1024]{1,0:T(8,128)(2,1)S(1)}, bf16[15,1024]{1,0:T(8,128)(2,1)S(1)}, u32[]{:S(2)}, u32[]{:S(2)}) collective-permute-start(bf16[15,1024]{1,0:T(8,128)(2,1)S(1)} %get-tuple-element.59), channel_id=1, source_target_pairs={{0,1},{1,2},{2,3},{3,4},{4,5},{5,6},{6,7},{7,8},{8,9},{9,10},{10,1... | collective-permute-start | bytes 92168 | tf_op jit(solution)/shard_map/ppermute | solution.py:20
  75.3 1.3 collective-permute-start.1
  76.8 2.2 %collective-permute-done.1 = bf16[15,1024]{1,0:T(8,128)(2,1)S(1)} collective-permute-done((bf16[15,1024]{1,0:T(8,128)(2,1)S(1)}, bf16[15,1024]{1,0:T(8,128)(2,1)S(1)}, u32[]{:S(2)}, u32[]{:S(2)}) %collective-permute-start.1) | collective-permute-done | bytes 30752 | tf_op jit(solution)/shard_map/ppermute | solution.py:23
  79.0 1.4 maximum_convert_fusion
  80.4 7.2 %fusion.88 = (f32[384]{0:T(512)S(1)}, f32[384,1024]{1,0:T(8,128)S(1)}) fusion(f32[1024]{0:T(1024)S(1)} %bitcast.179, f32[414,1024]{1,0:T(8,128)S(1)} %maximum_convert_fusion, f32[1024]{0:T(1024)S(1)} %bitcast.177, f32[1024]{0:T(1024)S(1)} %bitcast.175, f32[1024]{0:T(1024)S(1)} %bitcast.173, f32[1024]{0:T(1024)S(1)} %bitcast.171, f32[1024]{0:T(1024)S(1)} %bitcast.169, ...), kind=kLoop, calls=%fused_computation.186 | loop fusion | flops 24379008 | bytes 50460160 | tf_op jit(solution)/shard_map/reduce_sum | solution.py:29
  88.0 1.4 copy-done.4
  89.4 1.7 multiply_reduce_fusion
  91.1 4.6 %fusion.30 = (f32[1024]{0:T(1024)S(1)}, f32[1024]{0:T(1024)S(1)}, f32[1024]{0:T(1024)S(1)}, f32[1024]{0:T(1024)S(1)}, f32[1024]{0:T(1024)S(1)}, /*index=5*/f32[1...) fusion(f32[414,1024]{1,0:T(8,128)S(1)} %maximum_convert_fusion,, ...), kind=kLoop, calls=%fused_computation.63 | loop fusion | flops 17676288 | bytes 32327680 | tf_op jit(solution)/shard_map/reduce_sum | solution.py:391
  95.7 2.6 %fusion.29 = (f32[1024]{0:T(1024)S(1)}, f32[1024]{0:T(1024)S(1)}, f32[1024]{0:T(1024)S(1)}, f32[1024]{0:T(1024)S(1)}, f32[1024]{0:T(1024)S(1)}, /*index=5*/f32[1...) fusion(bf16[384,1024]{1,0:T(8,128)(2,1)S(1)} %get-tuple-element, ...), kind=kLoop, calls=%fused_computation.62 | loop fusion | flops 10603520 | bytes 21286912 | tf_op jit(solution)/shard_map/reduce_sum | solution.py:391
  98.4 4.5 %collective-permute-start.2 = (bf16[15,1024]{1,0:T(8,128)(2,1)S(1)}, bf16[15,1024]{1,0:T(8,128)(2,1)S(1)}, u32[]{:S(2)}, u32[]{:S(2)}) collective-permute-start(bf16[15,1024]{1,0:T(8,128)(2,1)S(1)} %get-tuple-element.57), channel_id=1, source_target_pairs={{0,1},{1,2},{2,3},{3,4},{4,5},{5,6},{6,7},{7,8},{8,9},{9,10},{10,1... | collective-permute-start | bytes 92168 | tf_op jit(solution)/shard_map/ppermute | solution.py:20
  102.9 1.5 collective-permute-start.3
  104.4 2.1 fusion.70
  106.8 6.7 %multiply_convert_fusion.1 = (bf16[384,1024]{1,0:T(8,128)(2,1)S(1)}, f32[384,1024]{1,0:T(8,128)S(1)}) fusion(f32[384,2048]{1,0:T(8,128)S(1)} %fusion.93, f32[384]{0:T(512)S(1)} %fusion.84, f32[1024]{0:T(1024)S(1)} %bitcast.180, f32[414,1024]{1,0:T(8,128)S(1)} %maximum_convert_fusion.1, f32[1024]{0:T(1024)S(1)} %bitcast.178, f32[1024]{0:T(1024)S(1)} %bitcast.176, ...), kind=kLoop, calls=%fused_computation.156 | loop fusion | flops 26345472 | bytes 52819456 | tf_op jit(solution)/shard_map/convert.1
  114.5 1.9 copy-done.10
  116.3 3.0 %fusion.82 = (f32[1024]{0:T(1024)S(1)}, f32[384]{0:T(512)S(1)}, f32[384]{0:T(512)S(1)}, bf16[384,1024]{1,0:T(8,128)(2,1)}, f32[384,1024]{1,0:T(8,128)S(1)}) fusion(bf16[16,24,1024]{2,1,0:T(8,128)(2,1)S(1)} %copy-done.1, f32[384]{0:T(512)S(1)} %rsqrt.22, f32[384]{0:T(512)S(1)} %div.41, f32[1024]{0:T(1024)S(1)} %copy-done.8, ...), kind=kOutput, calls=%fused_computation.153 | convolution fusion | flops 1618082048 | bytes 8927232 | tf_op jit(solution)/shard_map/dot_general | solution.py:404
  119.3 1.5 fusion.80
  120.8 5.9 %all-to-all-start.1 = ((bf16[16,24,1024]{2,1,0:T(8,128)(2,1)}), bf16[16,24,1024]{2,1,0:T(8,128)(2,1)S(1)}, u32[]{:S(2)}, u32[]{:S(2)}) async-start(bf16[16,24,1024]{2,1,0:T(8,128)(2,1)} %bitcast.37), calls=%async_computation.1 | async-start | bytes 1572864 | tf_op jit(solution)/shard_map/all_to_all | solution.py:418
  126.8 3.2 %convolution_convert_fusion.1 = bf16[1024,1024]{0,1:T(8,128)(2,1)S(1)} fusion(bf16[384,1024]{1,0:T(8,128)(2,1)} %param.9, f32[384,1024]{1,0:T(8,128)} %copy-done.2, f32[1024]{0:T(1024)S(1)} %copy-done.9, f32[384]{0:T(512)S(1)} %add_rsqrt_fusion.1, f32[384]{0:T(512)S(1)} %broadcast_multiply_fusion.7, f32[384]{0:T(512)S(1)} %fusion.84), kind=kOutput, calls=%fused_computation.32 | convolution fusion | flops 809893888 | bytes 4465152 | tf_op jit(solution)/shard_map/dot_general | solution.py:42
  131.2 4.0 %convolution_convert_fusion = bf16[2048,1024]{1,0:T(8,128)(2,1)S(1)} fusion(bf16[384,1024]{1,0:T(8,128)(2,1)} %get-tuple-element.56, bf16[384,1024]{1,0:T(8,128)(2,1)} %copy-done.5, bf16[384,1024]{1,0:T(8,128)(2,1)} %copy-done.6), kind=kOutput, calls=%fused_computation.31 | convolution fusion | flops 1615855616 | bytes 6553600 | tf_op jit(solution)/shard_map/dot_general | solution.py:42
  135.2 50.6 %reduce_rows.1 = (f32[128,1024]{1,0:T(8,128)S(1)}, f32[64,1024]{1,0:T(8,128)S(1)}) custom-call(bf16[8,2,128,1024]{3,2,1,0:T(8,128)(2,1)S(1)} %bitcast.115, bf16[8,2,64,1024]{3,2,1,0:T(8,128)(2,1)S(1)} %bitcast.116), custom_call_target="tpu_custom_call" | custom-call | flops 10000000 | bytes 120000000 | tf_op jit(solution)/shard_map/reduce_rows/pallas_call | solution.py:205
  187.4 24.1 %all_gather.3 = f32[384,128]{1,0:T(8,128)S(1)} all-gather(f32[24,128]{1,0:T(8,128)} %reduce-scatter.4.cloned.1.call-done), channel_id=1, replica_groups=mesh['groups'=2,'ctx'=16] {'ctx'}, dimensions={0}, use_global_device_ids=true | all-gather | bytes 208896 | tf_op jit(solution)/shard_map/all_gather | solution.py:415
  (61 shorter events, 8.9 us)
Async XLA Ops:
  7.2 59.5 %copy-start.7 = (bf16[1024,31]{0,1:T(8,128)(2,1)S(1)}, bf16[1024,31]{0,1:T(8,128)(2,1)}, u32[]{:S(2)}) copy-start(bf16[1024,31]{0,1:T(8,128)(2,1)} %param.13) | copy-start | bytes 190468
  7.2 60.2 %copy-start.8 = (f32[1024]{0:T(1024)S(1)}, f32[1024]{0:T(1024)}, u32[]{:S(2)}) copy-start(f32[1024]{0:T(1024)} %param.11) | copy-start | bytes 12292
  7.2 59.6 %all-to-all-start = ((bf16[16,24,1024]{2,1,0:T(8,128)(2,1)}), bf16[16,24,1024]{2,1,0:T(8,128)(2,1)S(1)}, u32[]{:S(2)}, u32[]{:S(2)}) async-start(bf16[16,24,1024]{2,1,0:T(8,128)(2,1)} %param.8), calls=%async_computation | async-start | bytes 1572864 | tf_op jit(solution)/shard_map/all_to_all | solution.py:349
  66.8 0.9 copy-start
  72.1 0.9 copy-start.3
  73.0 3.8 %collective-permute-start = (bf16[15,1024]{1,0:T(8,128)(2,1)S(1)}, bf16[15,1024]{1,0:T(8,128)(2,1)S(1)}, u32[]{:S(2)}, u32[]{:S(2)}) collective-permute-start(bf16[15,1024]{1,0:T(8,128)(2,1)S(1)} %get-tuple-element.59), channel_id=1, source_target_pairs={{0,1},{1,2},{2,3},{3,4},{4,5},{5,6},{6,7},{7,8},{8,9},{9,10},{10,1... | collective-permute-start | bytes 92168 | tf_op jit(solution)/shard_map/ppermute | solution.py:20
  75.3 3.7 %collective-permute-start.1 = (bf16[15,1024]{1,0:T(8,128)(2,1)S(1)}, bf16[15,1024]{1,0:T(8,128)(2,1)S(1)}, u32[]{:S(2)}, u32[]{:S(2)}) collective-permute-start(bf16[15,1024]{1,0:T(8,128)(2,1)S(1)} %get-tuple-element.60), channel_id=1, source_target_pairs={{1,0},{2,1},{3,2},{4,3},{5,4},{6,5},{7,6},{8,7},{9,8},{10,9},{11,1... | collective-permute-start | bytes 92168 | tf_op jit(solution)/shard_map/ppermute | solution.py:23
  80.4 7.6 %copy-start.11 = (bf16[8,2,64,1024]{3,2,1,0:T(8,128)(2,1)S(1)}, bf16[8,2,64,1024]{3,2,1,0:T(8,128)(2,1)}, u32[]{:S(2)}) copy-start(bf16[8,2,64,1024]{3,2,1,0:T(8,128)(2,1)} %get-tuple-element.11) | copy-start | bytes 6291460
  87.6 16.8 %copy-start.2 = (f32[384,1024]{1,0:T(8,128)}, f32[384,1024]{1,0:T(8,128)S(1)}, u32[]{:S(2)}) copy-start(f32[384,1024]{1,0:T(8,128)S(1)} %get-tuple-element.55) | copy-start | bytes 4718596
  87.7 1.7 copy-start.4
  87.7 1.7 copy-start.9
  95.7 8.7 %copy-start.1 = (bf16[16,24,1024]{2,1,0:T(8,128)(2,1)S(1)}, bf16[16,24,1024]{2,1,0:T(8,128)(2,1)}, u32[]{:S(2)}) copy-start(bf16[16,24,1024]{2,1,0:T(8,128)(2,1)} %copy-done) | copy-start | bytes 2359300
  98.4 8.2 %collective-permute-start.2 = (bf16[15,1024]{1,0:T(8,128)(2,1)S(1)}, bf16[15,1024]{1,0:T(8,128)(2,1)S(1)}, u32[]{:S(2)}, u32[]{:S(2)}) collective-permute-start(bf16[15,1024]{1,0:T(8,128)(2,1)S(1)} %get-tuple-element.57), channel_id=1, source_target_pairs={{0,1},{1,2},{2,3},{3,4},{4,5},{5,6},{6,7},{7,8},{8,9},{9,10},{10,1... | collective-permute-start | bytes 92168 | tf_op jit(solution)/shard_map/ppermute | solution.py:20
  102.9 3.6 %collective-permute-start.3 = (bf16[15,1024]{1,0:T(8,128)(2,1)S(1)}, bf16[15,1024]{1,0:T(8,128)(2,1)S(1)}, u32[]{:S(2)}, u32[]{:S(2)}) collective-permute-start(bf16[15,1024]{1,0:T(8,128)(2,1)S(1)} %get-tuple-element.58), channel_id=1, source_target_pairs={{1,0},{2,1},{3,2},{4,3},{5,4},{6,5},{7,6},{8,7},{9,8},{10,9},{11,1... | collective-permute-start | bytes 92168 | tf_op jit(solution)/shard_map/ppermute | solution.py:23
  113.6 0.9 copy-start.6
  113.6 2.8 %copy-start.10 = (bf16[8,2,128,1024]{3,2,1,0:T(8,128)(2,1)S(1)}, bf16[8,2,128,1024]{3,2,1,0:T(8,128)(2,1)}, u32[]{:S(2)}) copy-start(bf16[8,2,128,1024]{3,2,1,0:T(8,128)(2,1)} %get-tuple-element.10) | copy-start | bytes 12582916
  114.2 5.1 %copy-start.5 = (bf16[384,1024]{1,0:T(8,128)(2,1)}, bf16[384,1024]{1,0:T(8,128)(2,1)S(1)}, u32[]{:S(2)}) copy-start(bf16[384,1024]{1,0:T(8,128)(2,1)S(1)} %multiply_convert_fusion) | copy-start | bytes 2359300
  120.8 92.0 %all-to-all-start.1 = ((bf16[16,24,1024]{2,1,0:T(8,128)(2,1)}), bf16[16,24,1024]{2,1,0:T(8,128)(2,1)S(1)}, u32[]{:S(2)}, u32[]{:S(2)}) async-start(bf16[16,24,1024]{2,1,0:T(8,128)(2,1)} %bitcast.37), calls=%async_computation.1 | async-start | bytes 1572864 | tf_op jit(solution)/shard_map/all_to_all | solution.py:418
  126.8 60.6 %reduce-scatter.4.cloned.1.call-start = ((), (), s32[]{:S(2)}) async-start(), calls=%async_computation.3 | async-start | bytes 208896
Sparse Core Ops, SparseCore 0:
  131.3 55.8 reduce-scatter.3

commit v3 on v2

--- a/solution.py
+++ b/solution.py
@@ -109,9 +109,24 @@
 
 
 def reduce_kernel(
-    chips, first_ref, second_ref, first_out, second_out, outgoing, incoming, held, *sems
+    chips,
+    first_ref,
+    second_ref,
+    small_ref,
+    first_out,
+    second_out,
+    small_out,
+    outgoing,
+    incoming,
+    held,
+    pieces,
+    theirs,
+    slots,
+    totals,
+    *sems,
 ):
-    swap_send, swap_recv, ring_send, ring_recv = sems
+    swap_send, swap_recv, ring_send, ring_recv = sems[:4]
+    piece_send, piece_recv, slot_send, slot_recv = sems[4:]
     place, core, partner, right, left = position(chips)
     upper = first_ref.shape[2]
     rows = upper + second_ref.shape[2]
@@ -143,6 +158,33 @@
             device_id_type=MESH,
         )
 
+    def exchange(source, target, index):
+        return pltpu.make_async_remote_copy(
+            src_ref=source,
+            dst_ref=target,
+            send_sem=piece_send.at[index],
+            recv_sem=piece_recv.at[index],
+            device_id={"ctx": partner},
+            device_id_type=MESH,
+        )
+
+    def relay(way, step, arriving=False):
+        distance = step + 1 if arriving else step
+        ahead = place + distance if way else place + chips - distance
+        slot = slots.at[chip_at(lax.rem(ahead, chips), chips)]
+        return pltpu.make_async_remote_copy(
+            src_ref=slot,
+            dst_ref=slot,
+            send_sem=slot_send.at[way, step],
+            recv_sem=slot_recv.at[way, step],
+            device_id={"ctx": left if way else right},
+            device_id_type=MESH,
+        )
+
+    for side in range(2):
+        pieces[side] = small_ref[:, side * half : (side + 1) * half]
+    exchange(pieces.at[1 - core], theirs, 0).start()
+
     def give(step, carry):
         for way in range(2):
             columns = slice(way * half, (way + 1) * half)
@@ -173,13 +215,39 @@
             hop(way, step).start()
 
     lax.fori_loop(0, chips, give, 0)
+    exchange(pieces.at[1 - core], theirs, 0).wait_recv()
+    slots[chip_at(place, chips)] = (pieces[core] + theirs[...]).astype(slots.dtype)
     move(0, False)
+    for way in range(2):
+        relay(way, 0).start()
+    turn = chips // 2
+
+    def early(step, carry):
+        move(step, True)
+        for way in range(2):
+            relay(way, step - 1, True).wait_recv()
+            relay(way, step).start()
+        return carry
+
+    lax.fori_loop(1, turn - 1, early, 0)
+    move(turn - 1, True)
+    for way in range(2):
+        relay(way, turn - 2, True).wait_recv()
+    relay(0, turn - 1).start()
+    move(turn, True)
+    relay(0, turn - 1, True).wait_recv()
+
+    def add(chip, value):
+        return value + slots[chip].astype(jnp.float32)
+
+    totals[core] = lax.fori_loop(1, chips, add, slots[0].astype(jnp.float32))
+    exchange(totals.at[core], totals.at[core], 1).start()
 
     def middle(step, carry):
         move(step, True)
         return carry
 
-    lax.fori_loop(1, chips - 1, middle, 0)
+    lax.fori_loop(turn + 1, chips - 1, middle, 0)
     swap(chips - 1).wait_recv()
     for way in range(2):
         hop(way, chips - 2).wait_recv()
@@ -194,9 +262,22 @@
 
     lax.fori_loop(0, chips - 1, drain, 0)
     swap(chips - 1).wait_send()
-
-
-def reduce_rows(first, second, span):
+    exchange(totals.at[1 - core], totals.at[1 - core], 1).wait_recv()
+    for side in range(2):
+        small_out[:, side * half : (side + 1) * half] = totals[side]
+    exchange(pieces.at[1 - core], theirs, 0).wait_send()
+    exchange(totals.at[core], totals.at[core], 1).wait_send()
+
+    def settle(step, carry):
+        for way in range(2):
+            relay(way, step).wait_send()
+        return carry
+
+    lax.fori_loop(0, turn - 1, settle, 0)
+    relay(0, turn - 1).wait_send()
+
+
+def reduce_rows(first, second, small, span):
     chips = span // 2
     width = first.shape[1]
     upper, lower = first.shape[0] // span, second.shape[0] // span
@@ -207,24 +288,33 @@
         out_shape=(
             jax.ShapeDtypeStruct((upper, width), jnp.float32),
             jax.ShapeDtypeStruct((lower, width), jnp.float32),
+            jax.ShapeDtypeStruct(small.shape, jnp.float32),
         ),
-        in_specs=[whole] * 2,
-        out_specs=(whole,) * 2,
+        in_specs=[whole] * 3,
+        out_specs=(whole,) * 3,
         scratch_shapes=[
             pltpu.VMEM((chips, rows, width), first.dtype),
             pltpu.VMEM((chips, rows, width), first.dtype),
             pltpu.VMEM((2, chips, rows, width // 2), first.dtype),
+            pltpu.VMEM((2, small.shape[0], width // 2), jnp.float32),
+            pltpu.VMEM((small.shape[0], width // 2), jnp.float32),
+            pltpu.VMEM((chips, small.shape[0], width // 2), first.dtype),
+            pltpu.VMEM((2, small.shape[0], width // 2), jnp.float32),
             pltpu.SemaphoreType.DMA((chips,)),
             pltpu.SemaphoreType.DMA((chips,)),
             pltpu.SemaphoreType.DMA((2, chips - 1)),
             pltpu.SemaphoreType.DMA((2, chips - 1)),
+            pltpu.SemaphoreType.DMA((2,)),
+            pltpu.SemaphoreType.DMA((2,)),
+            pltpu.SemaphoreType.DMA((2, chips // 2)),
+            pltpu.SemaphoreType.DMA((2, chips // 2)),
         ],
         compiler_params=pltpu.CompilerParams(
             collective_id=0, has_side_effects=True, vmem_limit_bytes=44 * 2**20
         ),
         cost_estimate=pl.CostEstimate(flops=10**7, bytes_accessed=120 * 10**6, transcendentals=0),
         name="reduce_rows",
-    )(first.reshape(chips, 2, upper, width), second.reshape(chips, 2, lower, width))
+    )(first.reshape(chips, 2, upper, width), second.reshape(chips, 2, lower, width), small)
 
 
 def gather_kernel(
@@ -397,9 +487,6 @@
         [grad_glu * sigma, grad_glu * linear * sigma * (1.0 - sigma)], axis=1
     ).astype(jnp.bfloat16)
     partial_in = frame_sum(grad_projected, scaled_in).astype(sent)
-    rows_in, rows_out = reduce_rows(partial_in, partial_out, span)
-    grad_w_in = rows_in * scale
-    grad_w_out = rows_out * scale
     columns = grad_projected
     grad_scaled = jnp.dot(
         columns, whole_in, preferred_element_type=jnp.float32
@@ -411,8 +498,9 @@
     )
     blank = jnp.zeros((-(taps + 2) % 16, width), jnp.float32)
     small = jnp.concatenate([depth_local, gains_local, blank], axis=0)
-    small = lax.psum_scatter(small.reshape(-1, 128), "ctx", scatter_dimension=0, tiled=True)
-    small = lax.all_gather(small, "ctx", axis=0, tiled=True).reshape(-1, width)
+    rows_in, rows_out, small = reduce_rows(partial_in, partial_out, small, span)
+    grad_w_in = rows_in * scale
+    grad_w_out = rows_out * scale
     depth_total, gains_total = small[:taps].T, small[taps : taps + 2]
     grad_local = (grad_out.astype(jnp.float32) + grad_in).astype(jnp.bfloat16)
     grad_frames = lax.all_to_all(

time: 221 us -> 186 us (0.84)
  blocking collectives: 24.1 us -> 0 us
  between operations: 15.1 us -> 1.69 us
    all_gather x1 -> x0, blocking collectives: 24.1 us -> none  [shards(): small = lax.all_gather(small, 'ctx', axis=0, tiled=True).reshape(-1, width)]
    unnamed x25 -> x27, local copies, waits for them, and re-layouts: 5.26 us -> 6.45 us
  transfers between devices with their start and end apart: 7 -> 6, of which waited for: 1 -> 1; matrix products, arithmetic and copies ran while one was open for 6% -> 7% of each run, Pallas kernels for 46% -> 56%
where the time goes in v3:
time: 186 us
  Pallas kernels  104 us (56%)
  other arithmetic  29.4 us (16%)
  starting transfers between devices  23.2 us (12%)
  matrix products  17.8 us (10%)
  local copies, waits for them, and re-layouts  7.14 us (4%)
  waiting for transfers between devices  2.22 us (1%)
    pallas_call x1, Pallas kernels, reduce_rows(): pl.pallas_call(functools.partial(reduce_kernel, chips), out_shape=(jax.Sh...  52.8 us
    pallas_call x1, Pallas kernels, gather_rows(): pl.pallas_call(functools.partial(gather_kernel, chips), out_shape=(jax.Sh...  51.3 us
    all_to_all x1, starting transfers between devices, shards(): lax.all_to_all(frames, 'ctx', split_axis=0, concat_axis=1, tiled=True)  7.53 us
    reduce_sum x2, other arithmetic, normalize(): center = jnp.mean(values, axis=-1, keepdims=True)  7.41 us
    another operation x2, other arithmetic  7.37 us
    reduce_sum x2, other arithmetic, shards(): jnp.sum(grad_wide * padded[offset:offset + local_frames], axis=0)  7.26 us
    dot_general x2, matrix products, frame_sum(): lax.dot_general(left, right, (((0,), (0,)), ((), ())), preferred_element_...  6.99 us
    ppermute x2, starting transfers between devices, extended(): lax.ppermute(lax.slice_in_dim(block, block.shape[dim] - width, None, axis...  6.8 us
  transfers between devices with their start and end apart: 6, of which 1 were waited for; matrix products, arithmetic and copies ran while one was open for 7% of the time, Pallas kernels for 56%

profile of v3, /device:TPU:0, one launch (start us, length us, event | category | flops | bytes accessed | tf_op | source)
XLA Modules:
  0.0 185.5 jit_solution(10758929134794124480)
XLA Ops:
  0.7 7.5 %all-to-all-start = ((bf16[16,24,1024]{2,1,0:T(8,128)(2,1)}), bf16[16,24,1024]{2,1,0:T(8,128)(2,1)S(1)}, u32[]{:S(2)}, u32[]{:S(2)}) async-start(bf16[16,24,1024]{2,1,0:T(8,128)(2,1)} %param.8), calls=%async_computation | async-start | bytes 1572864 | tf_op jit(solution)/shard_map/all_to_all | solution.py:439
  8.8 51.3 %gather_rows.1 = (bf16[8,2,128,1024]{3,2,1,0:T(8,128)(2,1)}, bf16[8,2,64,1024]{3,2,1,0:T(8,128)(2,1)}) custom-call(bf16[128,1024]{1,0:T(8,128)(2,1)} %first_ref.1, bf16[64,1024]{1,0:T(8,128)(2,1)} %second_ref.1), custom_call_target="tpu_custom_call" | custom-call | flops 10000000 | bytes 120000000 | tf_op jit(solution)/shard_map/gather_rows/pallas_call | solution.py:420
  61.1 4.0 %fusion.93 = f32[384,2048]{1,0:T(8,128)S(1)} fusion(bf16[384,1024]{1,0:T(8,128)(2,1)S(1)} %bitcast.117, bf16[2048,1024]{1,0:T(8,128)(2,1)} %bitcast.213), kind=kOutput, calls=%fused_computation.191 | convolution fusion | flops 1610612736 | bytes 8126464 | tf_op jit(solution)/shard_map/dot_general | solution.py:48
  66.5 2.3 %collective-permute-start = (bf16[15,1024]{1,0:T(8,128)(2,1)S(1)}, bf16[15,1024]{1,0:T(8,128)(2,1)S(1)}, u32[]{:S(2)}, u32[]{:S(2)}) collective-permute-start(bf16[15,1024]{1,0:T(8,128)(2,1)S(1)} %get-tuple-element.61), channel_id=1, source_target_pairs={{0,1},{1,2},{2,3},{3,4},{4,5},{5,6},{6,7},{7,8},{8,9},{9,10},{10,1... | collective-permute-start | bytes 92168 | tf_op jit(solution)/shard_map/ppermute | solution.py:20
  68.7 1.3 collective-permute-start.1
  70.3 2.2 %collective-permute-done.1 = bf16[15,1024]{1,0:T(8,128)(2,1)S(1)} collective-permute-done((bf16[15,1024]{1,0:T(8,128)(2,1)S(1)}, bf16[15,1024]{1,0:T(8,128)(2,1)S(1)}, u32[]{:S(2)}, u32[]{:S(2)}) %collective-permute-start.1) | collective-permute-done | bytes 30752 | tf_op jit(solution)/shard_map/ppermute | solution.py:23
  72.5 1.4 maximum_convert_fusion
  73.9 7.2 %fusion.88 = (f32[384]{0:T(512)S(1)}, f32[384,1024]{1,0:T(8,128)S(1)}) fusion(f32[1024]{0:T(1024)S(1)} %bitcast.178, f32[414,1024]{1,0:T(8,128)S(1)} %maximum_convert_fusion, f32[1024]{0:T(1024)S(1)} %bitcast.176, f32[1024]{0:T(1024)S(1)} %bitcast.174, f32[1024]{0:T(1024)S(1)} %bitcast.172, f32[1024]{0:T(1024)S(1)} %bitcast.170, f32[1024]{0:T(1024)S(1)} %bitcast.168, ...), kind=kLoop, calls=%fused_computation.186 | loop fusion | flops 24379008 | bytes 50460160 | tf_op jit(solution)/shard_map/reduce_sum | solution.py:29
  81.5 1.4 copy-done.4
  82.8 1.7 multiply_reduce_fusion
  84.6 4.6 %fusion.30 = (f32[1024]{0:T(1024)S(1)}, f32[1024]{0:T(1024)S(1)}, f32[1024]{0:T(1024)S(1)}, f32[1024]{0:T(1024)S(1)}, f32[1024]{0:T(1024)S(1)}, /*index=5*/f32[1...) fusion(f32[414,1024]{1,0:T(8,128)S(1)} %maximum_convert_fusion,, ...), kind=kLoop, calls=%fused_computation.63 | loop fusion | flops 17676288 | bytes 32327680 | tf_op jit(solution)/shard_map/reduce_sum | solution.py:481
  89.2 2.6 %fusion.29 = (f32[1024]{0:T(1024)S(1)}, f32[1024]{0:T(1024)S(1)}, f32[1024]{0:T(1024)S(1)}, f32[1024]{0:T(1024)S(1)}, f32[1024]{0:T(1024)S(1)}, /*index=5*/f32[1...) fusion(bf16[384,1024]{1,0:T(8,128)(2,1)S(1)} %get-tuple-element, ...), kind=kLoop, calls=%fused_computation.62 | loop fusion | flops 10603520 | bytes 21286912 | tf_op jit(solution)/shard_map/reduce_sum | solution.py:481
  91.9 4.5 %collective-permute-start.2 = (bf16[15,1024]{1,0:T(8,128)(2,1)S(1)}, bf16[15,1024]{1,0:T(8,128)(2,1)S(1)}, u32[]{:S(2)}, u32[]{:S(2)}) collective-permute-start(bf16[15,1024]{1,0:T(8,128)(2,1)S(1)} %get-tuple-element.59), channel_id=1, source_target_pairs={{0,1},{1,2},{2,3},{3,4},{4,5},{5,6},{6,7},{7,8},{8,9},{9,10},{10,1... | collective-permute-start | bytes 92168 | tf_op jit(solution)/shard_map/ppermute | solution.py:20
  96.4 1.5 collective-permute-start.3
  97.9 2.1 %fusion.70 = bf16[384,1024]{1,0:T(8,128)(2,1)} fusion(bf16[16,24,1024]{2,1,0:T(8,128)(2,1)S(1)} %copy-done.1, bf16[1024,1024]{1,0:T(8,128)(2,1)S(1)} %bitcast.216, f32[384,1024]{1,0:T(8,128)S(1)} %get-tuple-element.57, f32[1024]{0:T(1024)S(1)} %copy-done.10, f32[384]{0:T(512)S(1)} %add_rsqrt_fusion.1, f32[384]{0:T(512)S(1)} %broadcast_multiply_fusion.7, ...), kind=kOutput, calls=%fused_computation.141 | convolution fusion | flops 810024960 | bytes 5251584 | tf_op jit(solution)/shard_map/dot_general | solution.py:48
  100.3 6.7 %multiply_convert_fusion.1 = (bf16[384,1024]{1,0:T(8,128)(2,1)S(1)}, f32[384,1024]{1,0:T(8,128)S(1)}) fusion(f32[384,2048]{1,0:T(8,128)S(1)} %fusion.93, f32[384]{0:T(512)S(1)} %fusion.84, f32[1024]{0:T(1024)S(1)} %bitcast.179, f32[414,1024]{1,0:T(8,128)S(1)} %maximum_convert_fusion.1, f32[1024]{0:T(1024)S(1)} %bitcast.177, f32[1024]{0:T(1024)S(1)} %bitcast.175, ...), kind=kLoop, calls=%fused_computation.156 | loop fusion | flops 26345472 | bytes 52819456 | tf_op jit(solution)/shard_map/convert.1
  107.9 1.9 %copy-done.11 = bf16[8,2,128,1024]{3,2,1,0:T(8,128)(2,1)S(1)} copy-done((bf16[8,2,128,1024]{3,2,1,0:T(8,128)(2,1)S(1)}, bf16[8,2,128,1024]{3,2,1,0:T(8,128)(2,1)}, u32[]{:S(2)}) %copy-start.11) | copy-done | bytes 4194328
  109.8 3.0 %fusion.82 = (f32[1024]{0:T(1024)S(1)}, f32[384]{0:T(512)S(1)}, f32[384]{0:T(512)S(1)}, bf16[384,1024]{1,0:T(8,128)(2,1)}, f32[384,1024]{1,0:T(8,128)S(1)}) fusion(bf16[16,24,1024]{2,1,0:T(8,128)(2,1)S(1)} %copy-done.1, f32[384]{0:T(512)S(1)} %rsqrt.22, f32[384]{0:T(512)S(1)} %div.41, f32[1024]{0:T(1024)S(1)} %copy-done.9, ...), kind=kOutput, calls=%fused_computation.153 | convolution fusion | flops 1618082048 | bytes 8927232 | tf_op jit(solution)/shard_map/dot_general | solution.py:491
  112.8 1.5 fusion.80
  114.3 6.1 %all-to-all-start.1 = ((bf16[16,24,1024]{2,1,0:T(8,128)(2,1)}), bf16[16,24,1024]{2,1,0:T(8,128)(2,1)}, u32[]{:S(2)}, u32[]{:S(2)}) async-start(bf16[16,24,1024]{2,1,0:T(8,128)(2,1)} %bitcast.37), calls=%async_computation.1 | async-start | bytes 1572864 | tf_op jit(solution)/shard_map/all_to_all | solution.py:506
  120.4 3.0 %convolution_convert_fusion.1 = bf16[1024,1024]{0,1:T(8,128)(2,1)S(1)} fusion(bf16[384,1024]{1,0:T(8,128)(2,1)S(1)} %copy-done.5, f32[384,1024]{1,0:T(8,128)} %copy-done.2, f32[1024]{0:T(1024)S(1)} %copy-done.10, f32[384]{0:T(512)S(1)} %add_rsqrt_fusion.1, f32[384]{0:T(512)S(1)} %broadcast_multiply_fusion.7, f32[384]{0:T(512)S(1)} %fusion.84), kind=kOutput, calls=%fused_computation.32 | convolution fusion | flops 809893888 | bytes 4465152 | tf_op jit(solution)/shard_map/dot_general | solution.py:42
  123.9 4.0 %convolution_convert_fusion = bf16[2048,1024]{1,0:T(8,128)(2,1)S(1)} fusion(bf16[384,1024]{1,0:T(8,128)(2,1)} %get-tuple-element.58, bf16[384,1024]{1,0:T(8,128)(2,1)} %copy-done.6, bf16[384,1024]{1,0:T(8,128)(2,1)} %copy-done.7), kind=kOutput, calls=%fused_computation.31 | convolution fusion | flops 1615855616 | bytes 6553600 | tf_op jit(solution)/shard_map/dot_general | solution.py:42
  127.8 52.8 %reduce_rows.1 = (f32[128,1024]{1,0:T(8,128)S(1)}, f32[64,1024]{1,0:T(8,128)S(1)}, f32[48,1024]{1,0:T(8,128)S(1)}) custom-call(bf16[8,2,128,1024]{3,2,1,0:T(8,128)(2,1)S(1)} %bitcast.115, bf16[8,2,64,1024]{3,2,1,0:T(8,128)(2,1)S(1)} %bitcast.116, f32[48,1024]{1,0:T(8,128)S(1)} %concatenate.16.small_ref), custom_call_target="tpu_custom_call" | custom-call | flops 10000000 | bytes 120000000 | tf_op jit(solution)/shard_map/reduce_rows/pallas_call | solution.py:286
  183.5 2.1 %copy.16 = bf16[16,24,1024]{2,1,0:T(8,128)(2,1)} copy(bf16[16,24,1024]{2,1,0:T(8,128)(2,1)} %all-to-all-done.1) | data formatting | bytes 1572864
  (56 shorter events, 7.2 us)
Async XLA Ops:
  0.6 59.5 %copy-start.8 = (bf16[1024,31]{0,1:T(8,128)(2,1)S(1)}, bf16[1024,31]{0,1:T(8,128)(2,1)}, u32[]{:S(2)}) copy-start(bf16[1024,31]{0,1:T(8,128)(2,1)} %param.13) | copy-start | bytes 190468
  0.6 60.2 %copy-start.9 = (f32[1024]{0:T(1024)S(1)}, f32[1024]{0:T(1024)}, u32[]{:S(2)}) copy-start(f32[1024]{0:T(1024)} %param.11) | copy-start | bytes 12292
  0.7 59.6 %all-to-all-start = ((bf16[16,24,1024]{2,1,0:T(8,128)(2,1)}), bf16[16,24,1024]{2,1,0:T(8,128)(2,1)S(1)}, u32[]{:S(2)}, u32[]{:S(2)}) async-start(bf16[16,24,1024]{2,1,0:T(8,128)(2,1)} %param.8), calls=%async_computation | async-start | bytes 1572864 | tf_op jit(solution)/shard_map/all_to_all | solution.py:439
  60.2 0.9 copy-start
  65.6 0.9 copy-start.3
  66.5 3.8 %collective-permute-start = (bf16[15,1024]{1,0:T(8,128)(2,1)S(1)}, bf16[15,1024]{1,0:T(8,128)(2,1)S(1)}, u32[]{:S(2)}, u32[]{:S(2)}) collective-permute-start(bf16[15,1024]{1,0:T(8,128)(2,1)S(1)} %get-tuple-element.61), channel_id=1, source_target_pairs={{0,1},{1,2},{2,3},{3,4},{4,5},{5,6},{6,7},{7,8},{8,9},{9,10},{10,1... | collective-permute-start | bytes 92168 | tf_op jit(solution)/shard_map/ppermute | solution.py:20
  68.7 3.7 %collective-permute-start.1 = (bf16[15,1024]{1,0:T(8,128)(2,1)S(1)}, bf16[15,1024]{1,0:T(8,128)(2,1)S(1)}, u32[]{:S(2)}, u32[]{:S(2)}) collective-permute-start(bf16[15,1024]{1,0:T(8,128)(2,1)S(1)} %get-tuple-element.62), channel_id=1, source_target_pairs={{1,0},{2,1},{3,2},{4,3},{5,4},{6,5},{7,6},{8,7},{9,8},{10,9},{11,1... | collective-permute-start | bytes 92168 | tf_op jit(solution)/shard_map/ppermute | solution.py:23
  73.9 7.6 %copy-start.12 = (bf16[8,2,64,1024]{3,2,1,0:T(8,128)(2,1)S(1)}, bf16[8,2,64,1024]{3,2,1,0:T(8,128)(2,1)}, u32[]{:S(2)}) copy-start(bf16[8,2,64,1024]{3,2,1,0:T(8,128)(2,1)} %get-tuple-element.12) | copy-start | bytes 6291460
  81.1 16.8 %copy-start.2 = (f32[384,1024]{1,0:T(8,128)}, f32[384,1024]{1,0:T(8,128)S(1)}, u32[]{:S(2)}) copy-start(f32[384,1024]{1,0:T(8,128)S(1)} %get-tuple-element.57) | copy-start | bytes 4718596
  81.1 1.7 copy-start.4
  81.1 1.7 copy-start.10
  89.2 8.7 %copy-start.1 = (bf16[16,24,1024]{2,1,0:T(8,128)(2,1)S(1)}, bf16[16,24,1024]{2,1,0:T(8,128)(2,1)}, u32[]{:S(2)}) copy-start(bf16[16,24,1024]{2,1,0:T(8,128)(2,1)} %copy-done) | copy-start | bytes 2359300
  91.9 8.2 %collective-permute-start.2 = (bf16[15,1024]{1,0:T(8,128)(2,1)S(1)}, bf16[15,1024]{1,0:T(8,128)(2,1)S(1)}, u32[]{:S(2)}, u32[]{:S(2)}) collective-permute-start(bf16[15,1024]{1,0:T(8,128)(2,1)S(1)} %get-tuple-element.59), channel_id=1, source_target_pairs={{0,1},{1,2},{2,3},{3,4},{4,5},{5,6},{6,7},{7,8},{8,9},{9,10},{10,1... | collective-permute-start | bytes 92168 | tf_op jit(solution)/shard_map/ppermute | solution.py:20
  96.4 3.6 %collective-permute-start.3 = (bf16[15,1024]{1,0:T(8,128)(2,1)S(1)}, bf16[15,1024]{1,0:T(8,128)(2,1)S(1)}, u32[]{:S(2)}, u32[]{:S(2)}) collective-permute-start(bf16[15,1024]{1,0:T(8,128)(2,1)S(1)} %get-tuple-element.60), channel_id=1, source_target_pairs={{1,0},{2,1},{3,2},{4,3},{5,4},{6,5},{7,6},{8,7},{9,8},{10,9},{11,1... | collective-permute-start | bytes 92168 | tf_op jit(solution)/shard_map/ppermute | solution.py:23
  107.0 0.9 copy-start.7
  107.0 2.8 %copy-start.11 = (bf16[8,2,128,1024]{3,2,1,0:T(8,128)(2,1)S(1)}, bf16[8,2,128,1024]{3,2,1,0:T(8,128)(2,1)}, u32[]{:S(2)}) copy-start(bf16[8,2,128,1024]{3,2,1,0:T(8,128)(2,1)} %get-tuple-element.11) | copy-start | bytes 12582916
  107.7 5.1 %copy-start.6 = (bf16[384,1024]{1,0:T(8,128)(2,1)}, bf16[384,1024]{1,0:T(8,128)(2,1)S(1)}, u32[]{:S(2)}) copy-start(bf16[384,1024]{1,0:T(8,128)(2,1)S(1)} %multiply_convert_fusion) | copy-start | bytes 2359300
  114.3 6.1 %copy-start.5 = (bf16[384,1024]{1,0:T(8,128)(2,1)S(1)}, bf16[384,1024]{1,0:T(8,128)(2,1)}, u32[]{:S(2)}) copy-start(bf16[384,1024]{1,0:T(8,128)(2,1)} %param.9) | copy-start | bytes 2359300
  114.3 69.2 %all-to-all-start.1 = ((bf16[16,24,1024]{2,1,0:T(8,128)(2,1)}), bf16[16,24,1024]{2,1,0:T(8,128)(2,1)}, u32[]{:S(2)}, u32[]{:S(2)}) async-start(bf16[16,24,1024]{2,1,0:T(8,128)(2,1)} %bitcast.37), calls=%async_computation.1 | async-start | bytes 1572864 | tf_op jit(solution)/shard_map/all_to_all | solution.py:506

commit v4 on v3

--- a/solution.py
+++ b/solution.py
@@ -111,10 +111,8 @@
 def reduce_kernel(
     chips,
     first_ref,
-    second_ref,
     small_ref,
     first_out,
-    second_out,
     small_out,
     outgoing,
     incoming,
@@ -128,10 +126,8 @@
     swap_send, swap_recv, ring_send, ring_recv = sems[:4]
     piece_send, piece_recv, slot_send, slot_recv = sems[4:]
     place, core, partner, right, left = position(chips)
-    upper = first_ref.shape[2]
-    rows = upper + second_ref.shape[2]
     half = first_ref.shape[3] // 2
-    parts = ((first_ref, first_out, 0, upper), (second_ref, second_out, upper, rows))
+    parts = ((first_ref, first_out, 0, first_ref.shape[2]),)
     greet((partner, right, left))
 
     def owner(way, step):
@@ -277,21 +273,19 @@
     relay(0, turn - 1).wait_send()
 
 
-def reduce_rows(first, second, small, span):
+def reduce_rows(first, small, span):
     chips = span // 2
     width = first.shape[1]
-    upper, lower = first.shape[0] // span, second.shape[0] // span
-    rows = upper + lower
+    rows = first.shape[0] // span
     whole = pl.BlockSpec(memory_space=pltpu.VMEM)
     return pl.pallas_call(
         functools.partial(reduce_kernel, chips),
         out_shape=(
-            jax.ShapeDtypeStruct((upper, width), jnp.float32),
-            jax.ShapeDtypeStruct((lower, width), jnp.float32),
+            jax.ShapeDtypeStruct((rows, width), jnp.float32),
             jax.ShapeDtypeStruct(small.shape, jnp.float32),
         ),
-        in_specs=[whole] * 3,
-        out_specs=(whole,) * 3,
+        in_specs=[whole] * 2,
+        out_specs=(whole,) * 2,
         scratch_shapes=[
             pltpu.VMEM((chips, rows, width), first.dtype),
             pltpu.VMEM((chips, rows, width), first.dtype),
@@ -314,17 +308,17 @@
         ),
         cost_estimate=pl.CostEstimate(flops=10**7, bytes_accessed=120 * 10**6, transcendentals=0),
         name="reduce_rows",
-    )(first.reshape(chips, 2, upper, width), second.reshape(chips, 2, lower, width), small)
+    )(first.reshape(chips, 2, rows, width), small)
 
 
 def gather_kernel(
-    chips, first_ref, second_ref, first_out, second_out, local, *sems
+    chips, first_ref, first_out, local, *sems
 ):
     ring_send, ring_recv, swap_send, swap_recv = sems
     place, core, partner, right, left = position(chips)
     last = chips // 2 - 1
     half = first_ref.shape[1] // 2
-    pairs = ((first_ref, first_out), (second_ref, second_out))
+    pairs = ((first_ref, first_out),)
     greet((partner, right, left))
 
     def block(which, way, step, side, cut):
@@ -367,15 +361,15 @@
             pairs[which][0], block(which, 0, 0, core, False), local.at[which]
         )
 
-    for which in range(2):
+    for which in range(1):
         for way in range(2):
             hop(which, way, 0, False, source=pairs[which][0]).start()
-    for which in range(2):
+    for which in range(1):
         swap(which, 0, 0, core, False, source=pairs[which][0]).start()
         keep(which).start()
 
     def forward(step, cut):
-        for which in range(2):
+        for which in range(1):
             for way in range(2):
                 hop(which, way, step - 1, False, arriving=True).wait_recv()
                 hop(which, way, step, cut).start()
@@ -387,13 +381,13 @@
 
     lax.fori_loop(1, last, middle, 0)
     forward(last, True)
-    for which in range(2):
+    for which in range(1):
         for way in range(2):
             hop(which, way, last, True, arriving=True).wait_recv()
             swap(which, way, last + 1, core, True).start()
 
     def drain(step, carry):
-        for which in range(2):
+        for which in range(1):
             for way in range(2):
                 hop(which, way, step, False).wait_send()
                 swap(which, way, step + 1, core, False).wait_send()
@@ -401,7 +395,7 @@
         return carry
 
     lax.fori_loop(0, last, drain, 0)
-    for which in range(2):
+    for which in range(1):
         keep(which).wait()
         swap(which, 0, 0, core, False, source=pairs[which][0]).wait_send()
         swap(which, 0, 0, 1 - core, False).wait_recv()
@@ -411,31 +405,29 @@
             swap(which, way, last + 1, 1 - core, True).wait_recv()
 
 
-def gather_rows(first, second, span):
+def gather_rows(first, span):
     chips = span // 2
     width = first.shape[1]
     kept = pl.BlockSpec(memory_space=pl.ANY)
-    ring = pltpu.SemaphoreType.DMA((2, 2, chips // 2))
-    swaps = pltpu.SemaphoreType.DMA((2, 2, chips // 2 + 1))
-    whole_first, whole_second = pl.pallas_call(
+    ring = pltpu.SemaphoreType.DMA((1, 2, chips // 2))
+    swaps = pltpu.SemaphoreType.DMA((1, 2, chips // 2 + 1))
+    whole = pl.pallas_call(
         functools.partial(gather_kernel, chips),
-        out_shape=(
-            jax.ShapeDtypeStruct((chips, 2) + first.shape, first.dtype),
-            jax.ShapeDtypeStruct((chips, 2) + second.shape, second.dtype),
-        ),
-        in_specs=[kept] * 2,
-        out_specs=(kept,) * 2,
-        scratch_shapes=[pltpu.SemaphoreType.DMA((2,)), ring, ring, swaps, swaps],
+        out_shape=jax.ShapeDtypeStruct((chips, 2) + first.shape, first.dtype),
+        in_specs=[kept],
+        out_specs=kept,
+        scratch_shapes=[pltpu.SemaphoreType.DMA((1,)), ring, ring, swaps, swaps],
         compiler_params=pltpu.CompilerParams(collective_id=1, has_side_effects=True),
         cost_estimate=pl.CostEstimate(flops=10**7, bytes_accessed=120 * 10**6, transcendentals=0),
         name="gather_rows",
-    )(first, second)
-    return (whole_first.reshape(-1, width), whole_second.reshape(-1, width))
+    )(first)
+    return whole.reshape(-1, width)
 
 
 def shards(frames, grad_out, valid_count, norm_gain, w_in, depth_weight, depth_gain, w_out):
     span = lax.axis_size("ctx")
-    whole_in, whole_out = gather_rows(w_in, w_out, span)
+    whole_in = gather_rows(w_in, span)
+    whole_out = lax.all_gather(w_out, "ctx", axis=0, tiled=True)
     ordered = lax.all_to_all(frames, "ctx", split_axis=0, concat_axis=1, tiled=True)
     local_frames = ordered.shape[1]
     width = ordered.shape[2]
@@ -463,6 +455,7 @@
     output = (wide_in + mixed).astype(jnp.bfloat16)
     sent = jnp.bfloat16 if span <= 32 else jnp.float32
     partial_out = frame_sum(grad_out, act).astype(sent)
+    rows_out = lax.psum_scatter(partial_out, "ctx", scatter_dimension=0, tiled=True)
     columns = grad_out
     grad_act = jnp.dot(
         columns,
@@ -498,9 +491,9 @@
     )
     blank = jnp.zeros((-(taps + 2) % 16, width), jnp.float32)
     small = jnp.concatenate([depth_local, gains_local, blank], axis=0)
-    rows_in, rows_out, small = reduce_rows(partial_in, partial_out, small, span)
+    rows_in, small = reduce_rows(partial_in, small, span)
     grad_w_in = rows_in * scale
-    grad_w_out = rows_out * scale
+    grad_w_out = rows_out.astype(jnp.float32) * scale
     depth_total, gains_total = small[:taps].T, small[taps : taps + 2]
     grad_local = (grad_out.astype(jnp.float32) + grad_in).astype(jnp.bfloat16)
     grad_frames = lax.all_to_all(

time: 186 us -> 211 us (1.13)
  between operations: 1.69 us -> 15.1 us
  local copies, waits for them, and re-layouts: 7.14 us -> 12.2 us
  matrix products: 17.8 us -> 22.1 us
  Pallas kernels: 104 us -> 107 us
    pallas_call x1, Pallas kernels: 51.3 us -> 57.5 us  [gather_rows(): pl.pallas_call(functools.partial(gather_kernel, chips), out_shape=jax.Sha...]
    unnamed x27 -> x32, local copies, waits for them, and re-layouts: 6.45 us -> 11.5 us
    pallas_call x1, Pallas kernels: 52.8 us -> 49.4 us  [reduce_rows(): pl.pallas_call(functools.partial(reduce_kernel, chips), out_shape=(jax.Sh...]
    dot_general x1, matrix products: 1.73 us -> 4.44 us  [shards(): grad_act = jnp.dot(columns, whole_out, preferred_element_type=jnp.float32)]
  transfers between devices with their start and end apart: 6 -> 8, of which waited for: 1 -> 1; matrix products, arithmetic and copies ran while one was open for 7% -> 27% of each run, Pallas kernels for 56% -> 51%
where the time goes in v4:
time: 211 us; the launch traced here: 210 us
  Pallas kernels  107 us (51%)
  other arithmetic  27.5 us (13%)
  starting transfers between devices  24.3 us (12%)
  matrix products  22.1 us (10%)
  between operations  15.1 us (7%)
  local copies, waits for them, and re-layouts  12.2 us (6%)
  waiting for transfers between devices  2.3 us (1%)
    pallas_call x1, Pallas kernels, gather_rows(): pl.pallas_call(functools.partial(gather_kernel, chips), out_shape=jax.Sha...  57.5 us
    pallas_call x1, Pallas kernels, reduce_rows(): pl.pallas_call(functools.partial(reduce_kernel, chips), out_shape=(jax.Sh...  49.4 us
    unnamed x32, local copies, waits for them, and re-layouts  11.5 us
    all_to_all x1, starting transfers between devices, shards(): lax.all_to_all(grad_local.reshape(frames.shape), 'ctx', split_axis=0, con...  7.73 us
    dot_general x2, matrix products, times_transposed(): lax.dot_general(left, right, (((1,), (1,)), ((), ())), preferred_element_...  7.7 us
    reduce_sum x2, other arithmetic, normalize(): center = jnp.mean(values, axis=-1, keepdims=True)  7.41 us
    all_to_all x1, starting transfers between devices, shards(): lax.all_to_all(frames, 'ctx', split_axis=0, concat_axis=1, tiled=True)  7.4 us
    another operation x2, other arithmetic  7.39 us
  transfers between devices with their start and end apart: 8, of which 1 were waited for; matrix products, arithmetic and copies ran while one was open for 27% of the time, Pallas kernels for 51%

profile of v4, /device:TPU:0, one launch (start us, length us, event | category | flops | bytes accessed | tf_op | source)
XLA Modules:
  0.0 210.4 jit_solution(9733562949722272416)
XLA Ops:
  7.2 7.4 %all-to-all-start = ((bf16[16,24,1024]{2,1,0:T(8,128)(2,1)}), bf16[16,24,1024]{2,1,0:T(8,128)(2,1)S(1)}, u32[]{:S(2)}, u32[]{:S(2)}) async-start(bf16[16,24,1024]{2,1,0:T(8,128)(2,1)} %param.8), calls=%async_computation | async-start | bytes 1572864 | tf_op jit(solution)/shard_map/all_to_all | solution.py:431
  16.0 57.5 %gather_rows.1 = bf16[8,2,128,1024]{3,2,1,0:T(8,128)(2,1)} custom-call(bf16[128,1024]{1,0:T(8,128)(2,1)} %first_ref.1), custom_call_target="tpu_custom_call" | custom-call | flops 10000000 | bytes 120000000 | tf_op jit(solution)/shard_map/gather_rows/pallas_call | solution.py:414
  74.5 4.0 %fusion.93 = f32[384,2048]{1,0:T(8,128)S(1)} fusion(bf16[384,1024]{1,0:T(8,128)(2,1)S(1)} %bitcast.116, bf16[2048,1024]{1,0:T(8,128)(2,1)} %bitcast.113), kind=kOutput, calls=%fused_computation.191 | convolution fusion | flops 1610612736 | bytes 8126464 | tf_op jit(solution)/shard_map/dot_general | solution.py:48
  79.0 1.2 copy-done
  80.2 2.3 %collective-permute-start = (bf16[15,1024]{1,0:T(8,128)(2,1)S(1)}, bf16[15,1024]{1,0:T(8,128)(2,1)S(1)}, u32[]{:S(2)}, u32[]{:S(2)}) collective-permute-start(bf16[15,1024]{1,0:T(8,128)(2,1)S(1)} %get-tuple-element.67), channel_id=1, source_target_pairs={{0,1},{1,2},{2,3},{3,4},{4,5},{5,6},{6,7},{7,8},{8,9},{9,10},{10,1... | collective-permute-start | bytes 92168 | tf_op jit(solution)/shard_map/ppermute | solution.py:20
  82.5 1.3 collective-permute-start.1
  84.0 1.6 collective-permute-done.1
  85.8 7.2 %fusion.88 = (f32[384]{0:T(512)S(1)}, f32[384,1024]{1,0:T(8,128)S(1)}) fusion(f32[1024]{0:T(1024)S(1)} %bitcast.177, f32[414,1024]{1,0:T(8,128)S(1)} %maximum_convert_fusion, f32[1024]{0:T(1024)S(1)} %bitcast.175, f32[1024]{0:T(1024)S(1)} %bitcast.173, f32[1024]{0:T(1024)S(1)} %bitcast.171, f32[1024]{0:T(1024)S(1)} %bitcast.169, f32[1024]{0:T(1024)S(1)} %bitcast.167, ...), kind=kLoop, calls=%fused_computation.186 | loop fusion | flops 24379008 | bytes 50460160 | tf_op jit(solution)/shard_map/reduce_sum | solution.py:29
  94.8 3.0 %convert_bitcast_fusion = bf16[1024,1024]{0,1:T(8,128)(2,1)} fusion(bf16[384,1024]{1,0:T(8,128)(2,1)S(1)} %copy-done.6, f32[384,1024]{1,0:T(8,128)S(1)} %get-tuple-element.63, f32[1024]{0:T(1024)S(1)} %copy-done.12, f32[384]{0:T(512)S(1)} %add_rsqrt_fusion.1, f32[384]{0:T(512)S(1)} %broadcast_multiply_fusion.6, f32[384]{0:T(512)S(1)} %fusion.84), kind=kOutput, calls=%fused_computation.32 | convolution fusion | flops 809893888 | bytes 4465152 | tf_op jit(solution)/shard_map/dot_general | solution.py:42
  97.8 3.9 %copy.16 = bf16[1024,1024]{1,0:T(8,128)(2,1)} copy(bf16[1024,1024]{0,1:T(8,128)(2,1)} %convert_bitcast_fusion) | data formatting | bytes 4194304
  101.8 4.4 %multiply_reduce_fusion = (f32[1024]{0:T(1024)}, f32[384]{0:T(512)S(1)}, f32[384]{0:T(512)S(1)}, f32[384,1024]{1,0:T(8,128)S(1)}) fusion(f32[384,1024]{1,0:T(8,128)} %copy-done.2, f32[384]{0:T(512)S(1)} %add_rsqrt_fusion.1, f32[384]{0:T(512)S(1)} %broadcast_multiply_fusion.6, f32[1024]{0:T(1024)S(1)} %copy-done.12, f32[384]{0:T(512)S(1)} %fusion.84, ...), kind=kOutput, calls=%fused_computation.153 | convolution fusion | flops 812382464 | bytes 6045184 | tf_op jit(solution)/shard_map/dot_general | solution.py:460
  106.2 4.5 %fusion.30 = (f32[1024]{0:T(1024)S(1)}, f32[1024]{0:T(1024)S(1)}, f32[1024]{0:T(1024)S(1)}, f32[1024]{0:T(1024)S(1)}, f32[1024]{0:T(1024)S(1)}, /*index=5*/f32[1...) fusion(f32[414,1024]{1,0:T(8,128)S(1)} %maximum_convert_fusion,, ...), kind=kLoop, calls=%fused_computation.63 | loop fusion | flops 17676288 | bytes 32327680 | tf_op jit(solution)/shard_map/reduce_sum | solution.py:474
  110.8 4.1 %collective-permute-start.2 = (bf16[15,1024]{1,0:T(8,128)(2,1)S(1)}, bf16[15,1024]{1,0:T(8,128)(2,1)S(1)}, u32[]{:S(2)}, u32[]{:S(2)}) collective-permute-start(bf16[15,1024]{1,0:T(8,128)(2,1)S(1)} %get-tuple-element.65), channel_id=1, source_target_pairs={{0,1},{1,2},{2,3},{3,4},{4,5},{5,6},{6,7},{7,8},{8,9},{9,10},{10,1... | collective-permute-start | bytes 92168 | tf_op jit(solution)/shard_map/ppermute | solution.py:20
  114.8 1.5 collective-permute-start.3
  116.3 2.6 %fusion.29 = (f32[1024]{0:T(1024)S(1)}, f32[1024]{0:T(1024)S(1)}, f32[1024]{0:T(1024)S(1)}, f32[1024]{0:T(1024)S(1)}, f32[1024]{0:T(1024)S(1)}, /*index=5*/f32[1...) fusion(bf16[384,1024]{1,0:T(8,128)(2,1)S(1)} %get-tuple-element, ...), kind=kLoop, calls=%fused_computation.62 | loop fusion | flops 10603520 | bytes 21286912 | tf_op jit(solution)/shard_map/reduce_sum | solution.py:474
  119.2 6.7 %multiply_convert_fusion.1 = (bf16[384,1024]{1,0:T(8,128)(2,1)S(1)}, f32[384,1024]{1,0:T(8,128)S(1)}) fusion(f32[384,2048]{1,0:T(8,128)S(1)} %copy-done.1, f32[384]{0:T(512)S(1)} %fusion.84, f32[1024]{0:T(1024)S(1)} %bitcast.178, f32[414,1024]{1,0:T(8,128)S(1)} %maximum_convert_fusion.1, f32[1024]{0:T(1024)S(1)} %bitcast.176, f32[1024]{0:T(1024)S(1)} %bitcast.174, ...), kind=kLoop, calls=%fused_computation.155 | loop fusion | flops 26345472 | bytes 52819456 | tf_op jit(solution)/shard_map/convert.1
  126.9 1.8 copy-done.5
  128.7 3.0 %fusion.82 = (f32[1024]{0:T(1024)S(1)}, f32[384]{0:T(512)S(1)}, f32[384]{0:T(512)S(1)}, bf16[384,1024]{1,0:T(8,128)(2,1)}, f32[384,1024]{1,0:T(8,128)S(1)}) fusion(bf16[16,24,1024]{2,1,0:T(8,128)(2,1)S(1)} %all-to-all-done, f32[384]{0:T(512)S(1)} %rsqrt.22, f32[384]{0:T(512)S(1)} %div.41, f32[1024]{0:T(1024)S(1)} %copy-done.10, ...), kind=kOutput, calls=%fused_computation.152 | convolution fusion | flops 1618082048 | bytes 8927232 | tf_op jit(solution)/shard_map/dot_general | solution.py:484
  131.7 1.5 fusion.80
  133.2 7.7 %all-to-all-start.1 = ((bf16[16,24,1024]{2,1,0:T(8,128)(2,1)}), bf16[16,24,1024]{2,1,0:T(8,128)(2,1)S(1)}, u32[]{:S(2)}, u32[]{:S(2)}) async-start(bf16[16,24,1024]{2,1,0:T(8,128)(2,1)} %bitcast.115), calls=%async_computation.1 | async-start | bytes 1572864 | tf_op jit(solution)/shard_map/all_to_all | solution.py:499
  141.0 3.7 %fusion.70 = bf16[384,1024]{1,0:T(8,128)(2,1)} fusion(bf16[16,24,1024]{2,1,0:T(8,128)(2,1)S(1)} %all-to-all-done, bf16[1024,1024]{1,0:T(8,128)(2,1)} %all-gather.2.cloned.1.call-done, f32[384,1024]{1,0:T(8,128)S(1)} %copy-done.4, f32[1024]{0:T(1024)S(1)} %copy-done.13, f32[384]{0:T(512)S(1)} %add_rsqrt_fusion.1, f32[384]{0:T(512)S(1)} %broadcast_multiply_fusion.6, ...), kind=kOutput, calls=%fused_computation.140 | convolution fusion | flops 810024960 | bytes 5251584 | tf_op jit(solution)/shard_map/dot_general | solution.py:48
  145.1 4.0 %convolution_convert_fusion = bf16[2048,1024]{1,0:T(8,128)(2,1)S(1)} fusion(bf16[384,1024]{1,0:T(8,128)(2,1)} %get-tuple-element.64, bf16[384,1024]{1,0:T(8,128)(2,1)} %copy-done.7, bf16[384,1024]{1,0:T(8,128)(2,1)} %copy-done.8), kind=kOutput, calls=%fused_computation.31 | convolution fusion | flops 1615855616 | bytes 6553600 | tf_op jit(solution)/shard_map/dot_general | solution.py:42
  149.1 49.4 %reduce_rows.1 = (f32[128,1024]{1,0:T(8,128)S(1)}, f32[48,1024]{1,0:T(8,128)S(1)}) custom-call(bf16[8,2,128,1024]{3,2,1,0:T(8,128)(2,1)S(1)} %bitcast.112, f32[48,1024]{1,0:T(8,128)S(1)} %concatenate.16.small_ref), custom_call_target="tpu_custom_call" | custom-call | flops 10000000 | bytes 120000000 | tf_op jit(solution)/shard_map/reduce_rows/pallas_call | solution.py:281
  200.7 1.1 copy.17
  (67 shorter events, 9.8 us)
Async XLA Ops:
  7.2 66.5 %all-to-all-start = ((bf16[16,24,1024]{2,1,0:T(8,128)(2,1)}), bf16[16,24,1024]{2,1,0:T(8,128)(2,1)S(1)}, u32[]{:S(2)}, u32[]{:S(2)}) async-start(bf16[16,24,1024]{2,1,0:T(8,128)(2,1)} %param.8), calls=%async_computation | async-start | bytes 1572864 | tf_op jit(solution)/shard_map/all_to_all | solution.py:431
  14.6 87.2 %all-gather.2.cloned.1.call-start = ((), (), s32[]{:S(2)}) async-start(), calls=%async_computation.3 | async-start | bytes 2228224 | tf_op jit(solution)/shard_map/all_gather | solution.py:430
  15.3 185.4 %reduce-scatter.4.cloned.1.call-start = ((), (), s32[]{:S(2)}) async-start(), calls=%async_computation.4 | async-start | bytes 2228224
  16.0 57.5 %copy-start.9 = (bf16[1024,31]{0,1:T(8,128)(2,1)S(1)}, bf16[1024,31]{0,1:T(8,128)(2,1)}, u32[]{:S(2)}) copy-start(bf16[1024,31]{0,1:T(8,128)(2,1)} %param.13) | copy-start | bytes 190468
  73.5 0.7 copy-start.10
  78.5 1.7 copy-start
  80.2 3.8 %collective-permute-start = (bf16[15,1024]{1,0:T(8,128)(2,1)S(1)}, bf16[15,1024]{1,0:T(8,128)(2,1)S(1)}, u32[]{:S(2)}, u32[]{:S(2)}) collective-permute-start(bf16[15,1024]{1,0:T(8,128)(2,1)S(1)} %get-tuple-element.67), channel_id=1, source_target_pairs={{0,1},{1,2},{2,3},{3,4},{4,5},{5,6},{6,7},{7,8},{8,9},{9,10},{10,1... | collective-permute-start | bytes 92168 | tf_op jit(solution)/shard_map/ppermute | solution.py:20
  82.5 3.1 %collective-permute-start.1 = (bf16[15,1024]{1,0:T(8,128)(2,1)S(1)}, bf16[15,1024]{1,0:T(8,128)(2,1)S(1)}, u32[]{:S(2)}, u32[]{:S(2)}) collective-permute-start(bf16[15,1024]{1,0:T(8,128)(2,1)S(1)} %get-tuple-element.68), channel_id=1, source_target_pairs={{1,0},{2,1},{3,2},{4,3},{5,4},{6,5},{7,6},{8,7},{9,8},{10,9},{11,1... | collective-permute-start | bytes 92168 | tf_op jit(solution)/shard_map/ppermute | solution.py:23
  93.1 1.1 copy-start.2
  93.1 1.7 copy-start.6
  93.1 1.7 copy-start.12
  101.8 4.5 %copy-start.3 = (f32[384,1024]{1,0:T(8,128)S(1)}, f32[384,1024]{1,0:T(8,128)}, u32[]{:S(2)}) copy-start(f32[384,1024]{1,0:T(8,128)} %copy-done.2) | copy-start | bytes 4718596
  110.8 8.2 %collective-permute-start.2 = (bf16[15,1024]{1,0:T(8,128)(2,1)S(1)}, bf16[15,1024]{1,0:T(8,128)(2,1)S(1)}, u32[]{:S(2)}, u32[]{:S(2)}) collective-permute-start(bf16[15,1024]{1,0:T(8,128)(2,1)S(1)} %get-tuple-element.65), channel_id=1, source_target_pairs={{0,1},{1,2},{2,3},{3,4},{4,5},{5,6},{6,7},{7,8},{8,9},{9,10},{10,1... | collective-permute-start | bytes 92168 | tf_op jit(solution)/shard_map/ppermute | solution.py:20
  114.8 4.1 %collective-permute-start.3 = (bf16[15,1024]{1,0:T(8,128)(2,1)S(1)}, bf16[15,1024]{1,0:T(8,128)(2,1)S(1)}, u32[]{:S(2)}, u32[]{:S(2)}) collective-permute-start(bf16[15,1024]{1,0:T(8,128)(2,1)S(1)} %get-tuple-element.66), channel_id=1, source_target_pairs={{1,0},{2,1},{3,2},{4,3},{5,4},{6,5},{7,6},{8,7},{9,8},{10,9},{11,1... | collective-permute-start | bytes 92168 | tf_op jit(solution)/shard_map/ppermute | solution.py:23
  116.3 2.9 %copy-start.1 = (f32[384,2048]{1,0:T(8,128)S(1)}, f32[384,2048]{1,0:T(8,128)}, u32[]{:S(2)}) copy-start(f32[384,2048]{1,0:T(8,128)} %copy-done) | copy-start | bytes 9437188
  126.0 0.9 copy-start.8
  126.0 2.8 %copy-start.5 = (bf16[8,2,128,1024]{3,2,1,0:T(8,128)(2,1)S(1)}, bf16[8,2,128,1024]{3,2,1,0:T(8,128)(2,1)}, u32[]{:S(2)}) copy-start(bf16[8,2,128,1024]{3,2,1,0:T(8,128)(2,1)} %gather_rows.1) | copy-start | bytes 12582916
  126.6 5.1 %copy-start.7 = (bf16[384,1024]{1,0:T(8,128)(2,1)}, bf16[384,1024]{1,0:T(8,128)(2,1)S(1)}, u32[]{:S(2)}) copy-start(bf16[384,1024]{1,0:T(8,128)(2,1)S(1)} %multiply_convert_fusion) | copy-start | bytes 2359300
  131.7 9.3 %copy-start.13 = (f32[1024]{0:T(1024)S(1)}, f32[1024]{0:T(1024)}, u32[]{:S(2)}) copy-start(f32[1024]{0:T(1024)} %param.14) | copy-start | bytes 12292
  133.2 7.8 %copy-start.4 = (f32[384,1024]{1,0:T(8,128)S(1)}, f32[384,1024]{1,0:T(8,128)}, u32[]{:S(2)}) copy-start(f32[384,1024]{1,0:T(8,128)} %copy-done.2) | copy-start | bytes 4718596
  133.2 69.4 %all-to-all-start.1 = ((bf16[16,24,1024]{2,1,0:T(8,128)(2,1)}), bf16[16,24,1024]{2,1,0:T(8,128)(2,1)S(1)}, u32[]{:S(2)}, u32[]{:S(2)}) async-start(bf16[16,24,1024]{2,1,0:T(8,128)(2,1)} %bitcast.115), calls=%async_computation.1 | async-start | bytes 1572864 | tf_op jit(solution)/shard_map/all_to_all | solution.py:499
  141.0 3.7 %copy-start.11 = (f32[1024]{0:T(1024)S(1)}, f32[1024]{0:T(1024)}, u32[]{:S(2)}) copy-start(f32[1024]{0:T(1024)} %get-tuple-element.22) | copy-start | bytes 12292
Sparse Core Ops, SparseCore 0:
  17.6 48.3 all-gather.1
  101.9 71.5 reduce-scatter.3
